TPU v7x, 768 devices: a whole 4x8x12 slice. The times are simulated.
768 devices in a mesh: ta: 12 (over z_hi, x), gz: 16 (over y, core), gy: 4 (over z_lo).
Axes of the slice: x: 4, y: 8, z: 12 (z_hi: 3, z_lo: 4; z = z_hi * 4 + z_lo), core: 2. Of those that a mesh axis runs over, the one named last changes fastest.
Arguments:
- source: float32 [4, 3, 2, 24, 16, 1024], P(None, None, None, 'ta', 'gz', 'gy'), may hold values from -6 to 6
- link_rows: float32 [4, 2, 3, 2, 24, 16, 1024], P(None, None, None, None, 'ta', 'gz', 'gy'), may hold values from -1 to 1, as said below
- clover_diag: float32 [2, 6, 24, 16, 1024], P(None, None, 'ta', 'gz', 'gy'), may hold values from 0.6 to 1.4
- clover_off: float32 [2, 15, 2, 24, 16, 1024], P(None, None, None, 'ta', 'gz', 'gy'), may hold values from -0.72 to 0.72
Outputs:
- solution: float32 [4, 3, 2, 24, 16, 1024], P(None, None, None, 'ta', 'gz', 'gy')
- residual: float32 [4, 3, 2, 24, 16, 1024], P(None, None, None, 'ta', 'gz', 'gy')
Inputs may be any that keep to these rules, and one draw needn't show every extreme that they name: `link_rows`: at every site and direction the two rows are the first two rows of a special unitary 3 x 3 matrix (real and imaginary parts along the fourth dimension).
All inputs are finite; a program needn't handle non-finite values.
Results may differ from a plain program's by a relative error of at most 0.000025.
Values sent between devices are 32-bit elements; how exact they have to be, the bound alone decides.
A program may use at most 32 MiB of HBM per device.

v0:
```python
import jax
import jax.numpy as jnp
from jax import lax
from jax.sharding import PartitionSpec as P

NX = 32
ITERS = 4


hop_weight = 0.125
damping = 0.8
UPPER_TABLE = (
    ((1, 0, 1), (0, 0, 1)),
    ((1, -1, 0), (0, 1, 0)),
    ((0, 0, 1), (1, 0, -1)),
    ((0, 1, 0), (1, 1, 0)),
)
LOWER_TABLE = (
    ((1, 0, -1), (0, 0, -1)),
    ((1, 1, 0), (0, -1, 0)),
    ((0, 0, -1), (1, 0, 1)),
    ((0, 1, 0), (1, 1, 0)),
)


def shifted(x, axis, by):
    devices = lax.axis_size(axis)
    return lax.ppermute(x, axis, [(i, (i + by) % devices) for i in range(devices)])


def padded_2(block, sides, width):
    for axis, dim in sides:
        count = lax.axis_size(axis)
        forward = [(i, i + 1) for i in range(count - 1)]
        forward.append((count - 1, 0))
        backward = [(target, source) for source, target in forward]
        low = lax.ppermute(
            lax.slice_in_dim(block, block.shape[dim] - width, None, axis=dim), axis, forward
        )
        high = lax.ppermute(lax.slice_in_dim(block, 0, width, axis=dim), axis, backward)
        block = jnp.concatenate([low, block, high], axis=dim)
    return block


def spin_mix(half, phase_table):
    rows_out = []
    for source_row, phase_real, phase_imag in phase_table:
        picked = half[source_row]
        real_part = picked[:, 0]
        imag_part = picked[:, 1]
        if phase_imag == 0:
            new_real = phase_real * real_part
            new_imag = phase_real * imag_part
        else:
            new_real = -phase_imag * imag_part
            new_imag = phase_imag * real_part
        rows_out.append(jnp.stack([new_real, new_imag], axis=1))
    return jnp.stack(rows_out, axis=0)


def spin_project(full_spinor, direction, factor):
    upper_half = full_spinor[0:2] + factor * spin_mix(full_spinor[2:4], UPPER_TABLE[direction])
    lower_half = full_spinor[2:4] + factor * spin_mix(full_spinor[0:2], LOWER_TABLE[direction])
    return jnp.concatenate([upper_half, lower_half], axis=0)


def full_link(rows):
    first_row = rows[0]
    second_row = rows[1]
    third = []
    for index in range(3):
        left = (index + 1) % 3
        right = (index + 2) % 3
        real_part = (
            first_row[left, 0] * second_row[right, 0]
            - first_row[left, 1] * second_row[right, 1]
            - first_row[right, 0] * second_row[left, 0]
            + first_row[right, 1] * second_row[left, 1]
        )
        imag_part = (
            first_row[left, 0] * second_row[right, 1]
            + first_row[left, 1] * second_row[right, 0]
            - first_row[right, 0] * second_row[left, 1]
            - first_row[right, 1] * second_row[left, 0]
        )
        third.append(jnp.stack([real_part, -imag_part], axis=0))
    return jnp.stack([first_row, second_row, jnp.stack(third, axis=0)], axis=0)


def color_times(link_field, vector, adjoint):
    real_out = 0.0
    imag_out = 0.0
    for column in range(3):
        if adjoint:
            link_real = link_field[column, :, 0]
            link_imag = -link_field[column, :, 1]
        else:
            link_real = link_field[:, column, 0]
            link_imag = link_field[:, column, 1]
        vector_real = vector[:, column, 0][:, None]
        vector_imag = vector[:, column, 1][:, None]
        real_out = real_out + link_real * vector_real - link_imag * vector_imag
        imag_out = imag_out + link_real * vector_imag + link_imag * vector_real
    return jnp.stack([real_out, imag_out], axis=2)


def clover_times(diagonal, offdiag, spinor):
    blocks = spinor.reshape((2, 6) + spinor.shape[2:])
    entries = [blocks[:, index] for index in range(6)]
    result = [diagonal[:, index][:, None] * entries[index] for index in range(6)]
    pair_index = 0
    for row_index in range(6):
        for second in range(row_index + 1, 6):
            real_part = offdiag[:, pair_index, 0]
            imag_part = offdiag[:, pair_index, 1]
            vector = entries[second]
            result[row_index] = result[row_index] + jnp.stack(
                [
                    real_part * vector[:, 0] - imag_part * vector[:, 1],
                    real_part * vector[:, 1] + imag_part * vector[:, 0],
                ],
                axis=1,
            )
            vector = entries[row_index]
            result[second] = result[second] + jnp.stack(
                [
                    real_part * vector[:, 0] + imag_part * vector[:, 1],
                    real_part * vector[:, 1] - imag_part * vector[:, 0],
                ],
                axis=1,
            )
            pair_index += 1
    return jnp.stack(result, axis=1).reshape(spinor.shape)


def row_ahead(field, row_cells):
    flat_cells = field.shape[-1]
    place_x = lax.broadcasted_iota(jnp.int32, (flat_cells,), 0) % row_cells
    return jnp.where(
        place_x == row_cells - 1,
        jnp.roll(field, row_cells - 1, axis=-1),
        jnp.roll(field, -1, axis=-1),
    )


def row_behind(field, row_cells):
    flat_cells = field.shape[-1]
    place_x = lax.broadcasted_iota(jnp.int32, (flat_cells,), 0) % row_cells
    return jnp.where(
        place_x == 0, jnp.roll(field, 1 - row_cells, axis=-1), jnp.roll(field, 1, axis=-1)
    )


def window_flat(padded, first_dim, along, offset, lengths, row_cells):
    starts = [1, 1, row_cells]
    steps_of = [1, 1, row_cells]
    starts[along] += offset * steps_of[along]
    for position in range(3):
        padded = lax.slice_in_dim(
            padded,
            starts[position],
            starts[position] + lengths[position],
            axis=first_dim + position,
        )
    return padded


def last_slab(rows, grid_dim, rim_width):
    extent = rows.shape[grid_dim]
    return lax.slice_in_dim(rows, extent - rim_width, extent, axis=grid_dim)


def behind_rows(rows, received, grid_dim, rim_width):
    extent = rows.shape[grid_dim]
    return jnp.concatenate(
        [received, lax.slice_in_dim(rows, 0, extent - rim_width, axis=grid_dim)], axis=grid_dim
    )


def body(source, link_rows, clover_diag, clover_off):
    layers = source.shape[3]
    depth_cells = source.shape[4]
    flat_cells = source.shape[5]
    row_cells = NX
    y_rows = flat_cells // row_cells
    cell_shape = (layers, depth_cells, y_rows, row_cells)
    lengths = (layers, depth_cells, flat_cells)
    link_fields = [full_link(link_rows[direction]) for direction in range(4)]
    place_t = lax.axis_index("ta")
    low_factor = jnp.where(place_t == 0, -1.0, 1.0).astype(jnp.float32)
    high_factor = jnp.where(place_t == lax.axis_size("ta") - 1, -1.0, 1.0).astype(jnp.float32)
    link_x = link_fields[0]
    link_x_behind = row_behind(link_x, row_cells)
    rows_y = link_rows[1]
    rows_z = link_rows[2]
    rows_t = link_rows[3]
    got_links_t = shifted(last_slab(rows_t, 3, 1), "ta", 1)
    got_links_z = shifted(last_slab(rows_z, 4, 1), "gz", 1)
    got_links_y = shifted(last_slab(rows_y, 5, row_cells), "gy", 1)
    behind_links = [
        full_link(behind_rows(rows_y, got_links_y, 5, row_cells)),
        full_link(behind_rows(rows_z, got_links_z, 4, 1)),
        full_link(behind_rows(rows_t, got_links_t, 3, 1)),
    ]
    grid_links = [link_fields[direction] for direction in range(1, 4)]
    layer_scale = jnp.concatenate(
        [low_factor[None], jnp.ones((layers,), jnp.float32), high_factor[None]]
    ).reshape(layers + 2, 1, 1)
    solution = source
    residual = source
    for sweep_index in range(ITERS):
        spinor_grid = solution.reshape((4, 3, 2) + cell_shape)
        padded = padded_2(spinor_grid, (("ta", 3), ("gz", 4), ("gy", 5)), 1)
        padded = (
            padded.reshape((4, 3, 2, layers + 2, depth_cells + 2, (y_rows + 2) * row_cells))
            * layer_scale
        )
        ahead_spinor = row_ahead(solution, row_cells)
        behind = row_behind(solution, row_cells)
        hopping = spin_project(color_times(link_x, ahead_spinor, False), 0, -1)
        hopping_hopping = hopping + spin_project(color_times(link_x_behind, behind, True), 0, 1)
        for hopping_direction in range(1, 4):
            along = 3 - hopping_direction
            hopping_ahead_spinor = window_flat(padded, 3, along, 1, lengths, row_cells)
            hopping_behind = window_flat(padded, 3, along, -1, lengths, row_cells)
            hopping_hopping = hopping_hopping + spin_project(
                color_times(grid_links[hopping_direction - 1], hopping_ahead_spinor, False),
                hopping_direction,
                -1,
            )
            hopping_hopping = hopping_hopping + spin_project(
                color_times(behind_links[hopping_direction - 1], hopping_behind, True),
                hopping_direction,
                1,
            )
        image = clover_times(clover_diag, clover_off, solution) - hop_weight * hopping_hopping
        residual = source - image
        solution = solution + damping * residual
    return (solution, residual)


def solution(mesh):
    in_specs = (
        P(None, None, None, "ta", "gz", "gy"),
        P(None, None, None, None, "ta", "gz", "gy"),
        P(None, None, "ta", "gz", "gy"),
        P(None, None, None, "ta", "gz", "gy"),
    )
    out_specs = (P(None, None, None, "ta", "gz", "gy"), P(None, None, None, "ta", "gz", "gy"))
    return jax.shard_map(body, mesh=mesh, in_specs=in_specs, out_specs=out_specs, check_vma=False)
```

profile of v0, /device:TPU:25, one launch (start us, length us, event | category | flops | bytes accessed | tf_op | source)
XLA Modules:
  0.0 223.4 jit_solution(2934662896082767977)
XLA Ops:
  1.8 16.5 %collective-permute-start.1 = (f32[4,3,2,1,1,8,32]{6,5,3,4,2,1,0:T(8,128)S(1)}, f32[4,3,2,1,1,8,32]{6,5,3,4,2,1,0:T(8,128)S(1)}, u32[]{:S(2)}, u32[]{:S(2)}) collective-permute-start(f32[4,3,2,1,1,8,32]{6,5,3,4,2,1,0:T(8,128)S(1)} %get-tuple-element.177), channel_id=1, source_target_pairs={{64,0},{128,64},{192,128},{256,192},{320,256},{384,320},{448,384},... | collective-permute-start | bytes 73736 | tf_op jit(solution)/shard_map/ppermute | solution.py:40
  18.3 1.9 collective-permute-start
  21.0 1.9 collective-permute-start.8
  22.9 3.4 %collective-permute-start.7 = (f32[2,3,2,2,1,256]{5,4,3,2,1,0:T(1,128)S(1)}, f32[2,3,2,2,1,256]{5,4,3,2,1,0:T(1,128)S(1)}, u32[]{:S(2)}, u32[]{:S(2)}) collective-permute-start(f32[2,3,2,2,1,256]{5,4,3,2,1,0:T(1,128)S(1)} %get-tuple-element.459), channel_id=1, source_target_pairs={{0,4},{4,8},{8,12},{12,16},{16,20},{20,24},{24,28},{28,32},{32,36}... | collective-permute-start | bytes 73736 | tf_op jit(solution)/shard_map/ppermute | solution.py:28
  26.4 3.1 %collective-permute-start.6 = (f32[2,3,2,2,1,32]{5,4,3,2,1,0:T(1,128)S(1)}, f32[2,3,2,2,1,32]{5,4,3,2,1,0:T(1,128)S(1)}, u32[]{:S(2)}, u32[]{:S(2)}) collective-permute-start(f32[2,3,2,2,1,32]{5,4,3,2,1,0:T(1,128)S(1)} %slice.5058), channel_id=1, source_target_pairs={{0,1},{1,2},{2,3},{3,0},{4,5},{5,6},{6,7},{7,4},{8,9},{9,10},{10,1... | collective-permute-start | bytes 9224 | tf_op jit(solution)/shard_map/ppermute | solution.py:28
  48.1 2.9 %collective-permute-start.2 = (f32[4,3,2,4,1,8,32]{6,5,3,4,2,1,0:T(8,128)S(1)}, f32[4,3,2,4,1,8,32]{6,5,3,4,2,1,0:T(8,128)S(1)}, u32[]{:S(2)}, u32[]{:S(2)}) collective-permute-start(f32[4,3,2,4,1,8,32]{6,5,3,4,2,1,0:T(8,128)S(1)} %pad_maximum_fusion.4), channel_id=1, source_target_pairs={{0,4},{4,8},{8,12},{12,16},{16,20},{20,24},{24,28},{28,32},{32,36}... | collective-permute-start | bytes 294920 | tf_op jit(solution)/shard_map/ppermute | solution.py:37
  51.3 5.3 %collective-permute-done.3 = f32[4,3,2,4,1,8,32]{6,5,3,4,2,1,0:T(8,128)S(1)} collective-permute-done((f32[4,3,2,4,1,8,32]{6,5,3,4,2,1,0:T(8,128)S(1)}, f32[4,3,2,4,1,8,32]{6,5,3,4,2,1,0:T(8,128)S(1)}, u32[]{:S(2)}, u32[]{:S(2)}) %collective-permute-start.3) | collective-permute-done | bytes 98336 | tf_op jit(solution)/shard_map/ppermute | solution.py:40
  56.7 4.0 %collective-permute-start.5 = (f32[4,3,2,4,3,1,32]{6,5,3,4,2,1,0:T(1,128)S(1)}, f32[4,3,2,4,3,1,32]{6,5,3,4,2,1,0:T(1,128)S(1)}, u32[]{:S(2)}, u32[]{:S(2)}) collective-permute-start(f32[4,3,2,4,3,1,32]{6,5,3,4,2,1,0:T(1,128)S(1)} %get-tuple-element.25), channel_id=1, source_target_pairs={{1,0},{2,1},{3,2},{0,3},{5,4},{6,5},{7,6},{4,7},{9,8},{10,9},{11,1... | collective-permute-start | bytes 110600 | tf_op jit(solution)/shard_map/ppermute | solution.py:40
  60.7 1.9 collective-permute-start.4
  64.2 4.7 %collective-permute-done.4 = f32[4,3,2,4,3,1,32]{6,5,3,4,2,1,0:T(1,128)S(1)} collective-permute-done((f32[4,3,2,4,3,1,32]{6,5,3,4,2,1,0:T(1,128)S(1)}, f32[4,3,2,4,3,1,32]{6,5,3,4,2,1,0:T(1,128)S(1)}, u32[]{:S(2)}, u32[]{:S(2)}) %collective-permute-start.4) | collective-permute-done | bytes 36896 | tf_op jit(solution)/shard_map/ppermute | solution.py:37
  74.5 9.7 %collective-permute-start.10 = (f32[4,3,2,1,1,8,32]{6,5,3,4,2,1,0:T(8,128)S(1)}, f32[4,3,2,1,1,8,32]{6,5,3,4,2,1,0:T(8,128)S(1)}, u32[]{:S(2)}, u32[]{:S(2)}) collective-permute-start(f32[4,3,2,1,1,8,32]{6,5,3,4,2,1,0:T(8,128)S(1)} %get-tuple-element.175), channel_id=1, source_target_pairs={{64,0},{128,64},{192,128},{256,192},{320,256},{384,320},{448,384},... | collective-permute-start | bytes 73736 | tf_op jit(solution)/shard_map/ppermute | solution.py:40
  84.2 2.1 collective-permute-start.9
  88.1 2.0 collective-permute-done.10
  90.1 12.0 %collective-permute-done.9 = f32[4,3,2,1,1,8,32]{6,5,3,4,2,1,0:T(8,128)S(1)} collective-permute-done((f32[4,3,2,1,1,8,32]{6,5,3,4,2,1,0:T(8,128)S(1)}, f32[4,3,2,1,1,8,32]{6,5,3,4,2,1,0:T(8,128)S(1)}, u32[]{:S(2)}, u32[]{:S(2)}) %collective-permute-start.9) | collective-permute-done | bytes 24608 | tf_op jit(solution)/shard_map/ppermute | solution.py:37
  102.5 2.5 %collective-permute-start.11 = (f32[4,3,2,4,1,8,32]{6,5,3,4,2,1,0:T(8,128)S(1)}, f32[4,3,2,4,1,8,32]{6,5,3,4,2,1,0:T(8,128)S(1)}, u32[]{:S(2)}, u32[]{:S(2)}) collective-permute-start(f32[4,3,2,4,1,8,32]{6,5,3,4,2,1,0:T(8,128)S(1)} %pad_maximum_fusion.5), channel_id=1, source_target_pairs={{0,4},{4,8},{8,12},{12,16},{16,20},{20,24},{24,28},{28,32},{32,36}... | collective-permute-start | bytes 294920 | tf_op jit(solution)/shard_map/ppermute | solution.py:37
  105.1 5.4 %collective-permute-done.12 = f32[4,3,2,4,1,8,32]{6,5,3,4,2,1,0:T(8,128)S(1)} collective-permute-done((f32[4,3,2,4,1,8,32]{6,5,3,4,2,1,0:T(8,128)S(1)}, f32[4,3,2,4,1,8,32]{6,5,3,4,2,1,0:T(8,128)S(1)}, u32[]{:S(2)}, u32[]{:S(2)}) %collective-permute-start.12) | collective-permute-done | bytes 98336 | tf_op jit(solution)/shard_map/ppermute | solution.py:40
  110.7 3.7 %collective-permute-start.14 = (f32[4,3,2,4,3,1,32]{6,5,3,4,2,1,0:T(1,128)S(1)}, f32[4,3,2,4,3,1,32]{6,5,3,4,2,1,0:T(1,128)S(1)}, u32[]{:S(2)}, u32[]{:S(2)}) collective-permute-start(f32[4,3,2,4,3,1,32]{6,5,3,4,2,1,0:T(1,128)S(1)} %get-tuple-element.23), channel_id=1, source_target_pairs={{1,0},{2,1},{3,2},{0,3},{5,4},{6,5},{7,6},{4,7},{9,8},{10,9},{11,1... | collective-permute-start | bytes 110600 | tf_op jit(solution)/shard_map/ppermute | solution.py:40
  114.4 1.9 collective-permute-start.13
  118.1 5.8 %collective-permute-done.13 = f32[4,3,2,4,3,1,32]{6,5,3,4,2,1,0:T(1,128)S(1)} collective-permute-done((f32[4,3,2,4,3,1,32]{6,5,3,4,2,1,0:T(1,128)S(1)}, f32[4,3,2,4,3,1,32]{6,5,3,4,2,1,0:T(1,128)S(1)}, u32[]{:S(2)}, u32[]{:S(2)}) %collective-permute-start.13) | collective-permute-done | bytes 36896 | tf_op jit(solution)/shard_map/ppermute | solution.py:37
  131.6 3.4 %collective-permute-start.15 = (f32[4,3,2,1,1,8,32]{6,5,3,4,2,1,0:T(8,128)S(1)}, f32[4,3,2,1,1,8,32]{6,5,3,4,2,1,0:T(8,128)S(1)}, u32[]{:S(2)}, u32[]{:S(2)}) collective-permute-start(f32[4,3,2,1,1,8,32]{6,5,3,4,2,1,0:T(8,128)S(1)} %get-tuple-element.172), channel_id=1, source_target_pairs={{0,64},{64,128},{128,192},{192,256},{256,320},{320,384},{384,448},... | collective-permute-start | bytes 73736 | tf_op jit(solution)/shard_map/ppermute | solution.py:37
  137.3 7.9 %collective-permute-done.15 = f32[4,3,2,1,1,8,32]{6,5,3,4,2,1,0:T(8,128)S(1)} collective-permute-done((f32[4,3,2,1,1,8,32]{6,5,3,4,2,1,0:T(8,128)S(1)}, f32[4,3,2,1,1,8,32]{6,5,3,4,2,1,0:T(8,128)S(1)}, u32[]{:S(2)}, u32[]{:S(2)}) %collective-permute-start.15) | collective-permute-done | bytes 24608 | tf_op jit(solution)/shard_map/ppermute | solution.py:37
  145.8 3.3 %collective-permute-start.17 = (f32[4,3,2,4,1,8,32]{6,5,3,4,2,1,0:T(8,128)S(1)}, f32[4,3,2,4,1,8,32]{6,5,3,4,2,1,0:T(8,128)S(1)}, u32[]{:S(2)}, u32[]{:S(2)}) collective-permute-start(f32[4,3,2,4,1,8,32]{6,5,3,4,2,1,0:T(8,128)S(1)} %pad_maximum_fusion.6), channel_id=1, source_target_pairs={{0,4},{4,8},{8,12},{12,16},{16,20},{20,24},{24,28},{28,32},{32,36}... | collective-permute-start | bytes 294920 | tf_op jit(solution)/shard_map/ppermute | solution.py:37
  149.0 5.4 %collective-permute-done.18 = f32[4,3,2,4,1,8,32]{6,5,3,4,2,1,0:T(8,128)S(1)} collective-permute-done((f32[4,3,2,4,1,8,32]{6,5,3,4,2,1,0:T(8,128)S(1)}, f32[4,3,2,4,1,8,32]{6,5,3,4,2,1,0:T(8,128)S(1)}, u32[]{:S(2)}, u32[]{:S(2)}) %collective-permute-start.18) | collective-permute-done | bytes 98336 | tf_op jit(solution)/shard_map/ppermute | solution.py:40
  154.7 7.3 %collective-permute-start.20 = (f32[4,3,2,4,3,1,32]{6,5,3,4,2,1,0:T(1,128)S(1)}, f32[4,3,2,4,3,1,32]{6,5,3,4,2,1,0:T(1,128)S(1)}, u32[]{:S(2)}, u32[]{:S(2)}) collective-permute-start(f32[4,3,2,4,3,1,32]{6,5,3,4,2,1,0:T(1,128)S(1)} %get-tuple-element.21), channel_id=1, source_target_pairs={{1,0},{2,1},{3,2},{0,3},{5,4},{6,5},{7,6},{4,7},{9,8},{10,9},{11,1... | collective-permute-start | bytes 110600 | tf_op jit(solution)/shard_map/ppermute | solution.py:40
  162.0 2.1 collective-permute-start.19
  165.7 5.8 %collective-permute-done.19 = f32[4,3,2,4,3,1,32]{6,5,3,4,2,1,0:T(1,128)S(1)} collective-permute-done((f32[4,3,2,4,3,1,32]{6,5,3,4,2,1,0:T(1,128)S(1)}, f32[4,3,2,4,3,1,32]{6,5,3,4,2,1,0:T(1,128)S(1)}, u32[]{:S(2)}, u32[]{:S(2)}) %collective-permute-start.19) | collective-permute-done | bytes 36896 | tf_op jit(solution)/shard_map/ppermute | solution.py:37
  179.2 3.4 %collective-permute-start.21 = (f32[4,3,2,1,1,8,32]{6,5,3,4,2,1,0:T(8,128)S(1)}, f32[4,3,2,1,1,8,32]{6,5,3,4,2,1,0:T(8,128)S(1)}, u32[]{:S(2)}, u32[]{:S(2)}) collective-permute-start(f32[4,3,2,1,1,8,32]{6,5,3,4,2,1,0:T(8,128)S(1)} %get-tuple-element.170), channel_id=1, source_target_pairs={{0,64},{64,128},{128,192},{192,256},{256,320},{320,384},{384,448},... | collective-permute-start | bytes 73736 | tf_op jit(solution)/shard_map/ppermute | solution.py:37
  184.9 6.9 %collective-permute-done.21 = f32[4,3,2,1,1,8,32]{6,5,3,4,2,1,0:T(8,128)S(1)} collective-permute-done((f32[4,3,2,1,1,8,32]{6,5,3,4,2,1,0:T(8,128)S(1)}, f32[4,3,2,1,1,8,32]{6,5,3,4,2,1,0:T(8,128)S(1)}, u32[]{:S(2)}, u32[]{:S(2)}) %collective-permute-start.21) | collective-permute-done | bytes 24608 | tf_op jit(solution)/shard_map/ppermute | solution.py:37
  192.8 4.4 %collective-permute-start.23 = (f32[4,3,2,4,1,8,32]{6,5,3,4,2,1,0:T(8,128)S(1)}, f32[4,3,2,4,1,8,32]{6,5,3,4,2,1,0:T(8,128)S(1)}, u32[]{:S(2)}, u32[]{:S(2)}) collective-permute-start(f32[4,3,2,4,1,8,32]{6,5,3,4,2,1,0:T(8,128)S(1)} %pad_maximum_fusion.7), channel_id=1, source_target_pairs={{0,4},{4,8},{8,12},{12,16},{16,20},{20,24},{24,28},{28,32},{32,36}... | collective-permute-start | bytes 294920 | tf_op jit(solution)/shard_map/ppermute | solution.py:37
  197.3 5.4 %collective-permute-done.24 = f32[4,3,2,4,1,8,32]{6,5,3,4,2,1,0:T(8,128)S(1)} collective-permute-done((f32[4,3,2,4,1,8,32]{6,5,3,4,2,1,0:T(8,128)S(1)}, f32[4,3,2,4,1,8,32]{6,5,3,4,2,1,0:T(8,128)S(1)}, u32[]{:S(2)}, u32[]{:S(2)}) %collective-permute-start.24) | collective-permute-done | bytes 98336 | tf_op jit(solution)/shard_map/ppermute | solution.py:40
  202.9 6.0 %collective-permute-start.26 = (f32[4,3,2,4,3,1,32]{6,5,3,4,2,1,0:T(1,128)S(1)}, f32[4,3,2,4,3,1,32]{6,5,3,4,2,1,0:T(1,128)S(1)}, u32[]{:S(2)}, u32[]{:S(2)}) collective-permute-start(f32[4,3,2,4,3,1,32]{6,5,3,4,2,1,0:T(1,128)S(1)} %get-tuple-element.19), channel_id=1, source_target_pairs={{1,0},{2,1},{3,2},{0,3},{5,4},{6,5},{7,6},{4,7},{9,8},{10,9},{11,1... | collective-permute-start | bytes 110600 | tf_op jit(solution)/shard_map/ppermute | solution.py:40
  212.6 5.8 %collective-permute-done.25 = f32[4,3,2,4,3,1,32]{6,5,3,4,2,1,0:T(1,128)S(1)} collective-permute-done((f32[4,3,2,4,3,1,32]{6,5,3,4,2,1,0:T(1,128)S(1)}, f32[4,3,2,4,3,1,32]{6,5,3,4,2,1,0:T(1,128)S(1)}, u32[]{:S(2)}, u32[]{:S(2)}) %collective-permute-start.25) | collective-permute-done | bytes 36896 | tf_op jit(solution)/shard_map/ppermute | solution.py:37
  (624 shorter events, 60.9 us)
Async XLA Ops:
  0.6 42.8 %copy-start.1 = (f32[4,3,2,2,1,256]{5,4,3,2,1,0:T(1,128)S(1)}, f32[4,3,2,2,1,256]{5,4,3,2,1,0:T(1,128)}, u32[]{:S(2)}) copy-start(f32[4,3,2,2,1,256]{5,4,3,2,1,0:T(1,128)} %param.4) | copy-start | bytes 147460
  0.6 43.9 %copy-start.10 = (f32[2,6,2,1,256]{4,3,2,1,0:T(1,128)S(1)}, f32[2,6,2,1,256]{4,3,2,1,0:T(1,128)}, u32[]{:S(2)}) copy-start(f32[2,6,2,1,256]{4,3,2,1,0:T(1,128)} %param.6) | copy-start | bytes 73732
  1.8 46.2 %collective-permute-start.1 = (f32[4,3,2,1,1,8,32]{6,5,3,4,2,1,0:T(8,128)S(1)}, f32[4,3,2,1,1,8,32]{6,5,3,4,2,1,0:T(8,128)S(1)}, u32[]{:S(2)}, u32[]{:S(2)}) collective-permute-start(f32[4,3,2,1,1,8,32]{6,5,3,4,2,1,0:T(8,128)S(1)} %get-tuple-element.177), channel_id=1, source_target_pairs={{64,0},{128,64},{192,128},{256,192},{320,256},{384,320},{448,384},... | collective-permute-start | bytes 73736 | tf_op jit(solution)/shard_map/ppermute | solution.py:40
  18.3 29.8 %collective-permute-start = (f32[4,3,2,1,1,8,32]{6,5,3,4,2,1,0:T(8,128)S(1)}, f32[4,3,2,1,1,8,32]{6,5,3,4,2,1,0:T(8,128)S(1)}, u32[]{:S(2)}, u32[]{:S(2)}) collective-permute-start(f32[4,3,2,1,1,8,32]{6,5,3,4,2,1,0:T(8,128)S(1)} %get-tuple-element.176), channel_id=1, source_target_pairs={{0,64},{64,128},{128,192},{192,256},{256,320},{320,384},{384,448},... | collective-permute-start | bytes 73736 | tf_op jit(solution)/shard_map/ppermute | solution.py:37
  21.0 26.8 %collective-permute-start.8 = (f32[2,3,2,1,1,256]{5,4,3,2,1,0:T(1,128)S(1)}, f32[2,3,2,1,1,256]{5,4,3,2,1,0:T(1,128)S(1)}, u32[]{:S(2)}, u32[]{:S(2)}) collective-permute-start(f32[2,3,2,1,1,256]{5,4,3,2,1,0:T(1,128)S(1)} %get-tuple-element.863), channel_id=1, source_target_pairs={{0,64},{64,128},{128,192},{192,256},{256,320},{320,384},{384,448},... | collective-permute-start | bytes 36872 | tf_op jit(solution)/shard_map/ppermute | solution.py:28
  22.9 28.2 %collective-permute-start.7 = (f32[2,3,2,2,1,256]{5,4,3,2,1,0:T(1,128)S(1)}, f32[2,3,2,2,1,256]{5,4,3,2,1,0:T(1,128)S(1)}, u32[]{:S(2)}, u32[]{:S(2)}) collective-permute-start(f32[2,3,2,2,1,256]{5,4,3,2,1,0:T(1,128)S(1)} %get-tuple-element.459), channel_id=1, source_target_pairs={{0,4},{4,8},{8,12},{12,16},{16,20},{20,24},{24,28},{28,32},{32,36}... | collective-permute-start | bytes 73736 | tf_op jit(solution)/shard_map/ppermute | solution.py:28
  26.4 21.0 %collective-permute-start.6 = (f32[2,3,2,2,1,32]{5,4,3,2,1,0:T(1,128)S(1)}, f32[2,3,2,2,1,32]{5,4,3,2,1,0:T(1,128)S(1)}, u32[]{:S(2)}, u32[]{:S(2)}) collective-permute-start(f32[2,3,2,2,1,32]{5,4,3,2,1,0:T(1,128)S(1)} %slice.5058), channel_id=1, source_target_pairs={{0,1},{1,2},{2,3},{3,0},{4,5},{5,6},{6,7},{7,4},{8,9},{9,10},{10,1... | collective-permute-start | bytes 9224 | tf_op jit(solution)/shard_map/ppermute | solution.py:28
  48.1 8.4 %collective-permute-start.3 = (f32[4,3,2,4,1,8,32]{6,5,3,4,2,1,0:T(8,128)S(1)}, f32[4,3,2,4,1,8,32]{6,5,3,4,2,1,0:T(8,128)S(1)}, u32[]{:S(2)}, u32[]{:S(2)}) collective-permute-start(f32[4,3,2,4,1,8,32]{6,5,3,4,2,1,0:T(8,128)S(1)} %pad_maximum_fusion.4), channel_id=1, source_target_pairs={{4,0},{8,4},{12,8},{16,12},{20,16},{24,20},{28,24},{32,28},{36,32}... | collective-permute-start | bytes 294920 | tf_op jit(solution)/shard_map/ppermute | solution.py:40
  48.1 8.4 %collective-permute-start.2 = (f32[4,3,2,4,1,8,32]{6,5,3,4,2,1,0:T(8,128)S(1)}, f32[4,3,2,4,1,8,32]{6,5,3,4,2,1,0:T(8,128)S(1)}, u32[]{:S(2)}, u32[]{:S(2)}) collective-permute-start(f32[4,3,2,4,1,8,32]{6,5,3,4,2,1,0:T(8,128)S(1)} %pad_maximum_fusion.4), channel_id=1, source_target_pairs={{0,4},{4,8},{8,12},{12,16},{16,20},{20,24},{24,28},{28,32},{32,36}... | collective-permute-start | bytes 294920 | tf_op jit(solution)/shard_map/ppermute | solution.py:37
  56.7 7.5 %collective-permute-start.5 = (f32[4,3,2,4,3,1,32]{6,5,3,4,2,1,0:T(1,128)S(1)}, f32[4,3,2,4,3,1,32]{6,5,3,4,2,1,0:T(1,128)S(1)}, u32[]{:S(2)}, u32[]{:S(2)}) collective-permute-start(f32[4,3,2,4,3,1,32]{6,5,3,4,2,1,0:T(1,128)S(1)} %get-tuple-element.25), channel_id=1, source_target_pairs={{1,0},{2,1},{3,2},{0,3},{5,4},{6,5},{7,6},{4,7},{9,8},{10,9},{11,1... | collective-permute-start | bytes 110600 | tf_op jit(solution)/shard_map/ppermute | solution.py:40
  60.7 8.1 %collective-permute-start.4 = (f32[4,3,2,4,3,1,32]{6,5,3,4,2,1,0:T(1,128)S(1)}, f32[4,3,2,4,3,1,32]{6,5,3,4,2,1,0:T(1,128)S(1)}, u32[]{:S(2)}, u32[]{:S(2)}) collective-permute-start(f32[4,3,2,4,3,1,32]{6,5,3,4,2,1,0:T(1,128)S(1)} %get-tuple-element.24), channel_id=1, source_target_pairs={{0,1},{1,2},{2,3},{3,0},{4,5},{5,6},{6,7},{7,4},{8,9},{9,10},{10,1... | collective-permute-start | bytes 110600 | tf_op jit(solution)/shard_map/ppermute | solution.py:37
  70.2 3.1 %copy-start = (f32[2,15,2,2,1,256]{5,4,3,2,1,0:T(1,128)S(1)}, f32[2,15,2,2,1,256]{5,4,3,2,1,0:T(1,128)}, u32[]{:S(2)}) copy-start(f32[2,15,2,2,1,256]{5,4,3,2,1,0:T(1,128)} %param.7) | copy-start | bytes 368644
  74.5 15.5 %collective-permute-start.10 = (f32[4,3,2,1,1,8,32]{6,5,3,4,2,1,0:T(8,128)S(1)}, f32[4,3,2,1,1,8,32]{6,5,3,4,2,1,0:T(8,128)S(1)}, u32[]{:S(2)}, u32[]{:S(2)}) collective-permute-start(f32[4,3,2,1,1,8,32]{6,5,3,4,2,1,0:T(8,128)S(1)} %get-tuple-element.175), channel_id=1, source_target_pairs={{64,0},{128,64},{192,128},{256,192},{320,256},{384,320},{448,384},... | collective-permute-start | bytes 73736 | tf_op jit(solution)/shard_map/ppermute | solution.py:40
  84.2 17.8 %collective-permute-start.9 = (f32[4,3,2,1,1,8,32]{6,5,3,4,2,1,0:T(8,128)S(1)}, f32[4,3,2,1,1,8,32]{6,5,3,4,2,1,0:T(8,128)S(1)}, u32[]{:S(2)}, u32[]{:S(2)}) collective-permute-start(f32[4,3,2,1,1,8,32]{6,5,3,4,2,1,0:T(8,128)S(1)} %get-tuple-element.174), channel_id=1, source_target_pairs={{0,64},{64,128},{128,192},{192,256},{256,320},{320,384},{384,448},... | collective-permute-start | bytes 73736 | tf_op jit(solution)/shard_map/ppermute | solution.py:37
  88.0 35.9 %copy-start.6 = (f32[2,6,2,2,1,256]{5,4,3,2,1,0:T(1,128)}, f32[2,6,2,2,1,256]{5,4,3,2,1,0:T(1,128)S(1)}, u32[]{:S(2)}) copy-start(f32[2,6,2,2,1,256]{5,4,3,2,1,0:T(1,128)S(1)} %constant_dynamic-update-slice_fusion.6) | copy-start | bytes 147460
  102.1 8.4 %collective-permute-start.12 = (f32[4,3,2,4,1,8,32]{6,5,3,4,2,1,0:T(8,128)S(1)}, f32[4,3,2,4,1,8,32]{6,5,3,4,2,1,0:T(8,128)S(1)}, u32[]{:S(2)}, u32[]{:S(2)}) collective-permute-start(f32[4,3,2,4,1,8,32]{6,5,3,4,2,1,0:T(8,128)S(1)} %pad_maximum_fusion.5), channel_id=1, source_target_pairs={{4,0},{8,4},{12,8},{16,12},{20,16},{24,20},{28,24},{32,28},{36,32}... | collective-permute-start | bytes 294920 | tf_op jit(solution)/shard_map/ppermute | solution.py:40
  102.5 8.0 %collective-permute-start.11 = (f32[4,3,2,4,1,8,32]{6,5,3,4,2,1,0:T(8,128)S(1)}, f32[4,3,2,4,1,8,32]{6,5,3,4,2,1,0:T(8,128)S(1)}, u32[]{:S(2)}, u32[]{:S(2)}) collective-permute-start(f32[4,3,2,4,1,8,32]{6,5,3,4,2,1,0:T(8,128)S(1)} %pad_maximum_fusion.5), channel_id=1, source_target_pairs={{0,4},{4,8},{8,12},{12,16},{16,20},{20,24},{24,28},{28,32},{32,36}... | collective-permute-start | bytes 294920 | tf_op jit(solution)/shard_map/ppermute | solution.py:37
  110.7 7.3 %collective-permute-start.14 = (f32[4,3,2,4,3,1,32]{6,5,3,4,2,1,0:T(1,128)S(1)}, f32[4,3,2,4,3,1,32]{6,5,3,4,2,1,0:T(1,128)S(1)}, u32[]{:S(2)}, u32[]{:S(2)}) collective-permute-start(f32[4,3,2,4,3,1,32]{6,5,3,4,2,1,0:T(1,128)S(1)} %get-tuple-element.23), channel_id=1, source_target_pairs={{1,0},{2,1},{3,2},{0,3},{5,4},{6,5},{7,6},{4,7},{9,8},{10,9},{11,1... | collective-permute-start | bytes 110600 | tf_op jit(solution)/shard_map/ppermute | solution.py:40
  114.4 9.5 %collective-permute-start.13 = (f32[4,3,2,4,3,1,32]{6,5,3,4,2,1,0:T(1,128)S(1)}, f32[4,3,2,4,3,1,32]{6,5,3,4,2,1,0:T(1,128)S(1)}, u32[]{:S(2)}, u32[]{:S(2)}) collective-permute-start(f32[4,3,2,4,3,1,32]{6,5,3,4,2,1,0:T(1,128)S(1)} %get-tuple-element.22), channel_id=1, source_target_pairs={{0,1},{1,2},{2,3},{3,0},{4,5},{5,6},{6,7},{7,4},{8,9},{9,10},{10,1... | collective-permute-start | bytes 110600 | tf_op jit(solution)/shard_map/ppermute | solution.py:37
  125.3 2.7 %copy-start.3 = (f32[2,3,2,2,1,256]{5,4,3,2,1,0:T(1,128)S(1)}, f32[2,3,2,2,1,256]{5,4,3,2,1,0:T(1,128)}, u32[]{:S(2)}) copy-start(f32[2,3,2,2,1,256]{5,4,3,2,1,0:T(1,128)} %get-tuple-element.650) | copy-start | bytes 73732
  129.6 7.4 %collective-permute-start.16 = (f32[4,3,2,1,1,8,32]{6,5,3,4,2,1,0:T(8,128)S(1)}, f32[4,3,2,1,1,8,32]{6,5,3,4,2,1,0:T(8,128)S(1)}, u32[]{:S(2)}, u32[]{:S(2)}) collective-permute-start(f32[4,3,2,1,1,8,32]{6,5,3,4,2,1,0:T(8,128)S(1)} %get-tuple-element.173), channel_id=1, source_target_pairs={{64,0},{128,64},{192,128},{256,192},{320,256},{384,320},{448,384},... | collective-permute-start | bytes 73736 | tf_op jit(solution)/shard_map/ppermute | solution.py:40
  131.6 13.6 %collective-permute-start.15 = (f32[4,3,2,1,1,8,32]{6,5,3,4,2,1,0:T(8,128)S(1)}, f32[4,3,2,1,1,8,32]{6,5,3,4,2,1,0:T(8,128)S(1)}, u32[]{:S(2)}, u32[]{:S(2)}) collective-permute-start(f32[4,3,2,1,1,8,32]{6,5,3,4,2,1,0:T(8,128)S(1)} %get-tuple-element.172), channel_id=1, source_target_pairs={{0,64},{64,128},{128,192},{192,256},{256,320},{320,384},{384,448},... | collective-permute-start | bytes 73736 | tf_op jit(solution)/shard_map/ppermute | solution.py:37
  145.2 9.3 %collective-permute-start.18 = (f32[4,3,2,4,1,8,32]{6,5,3,4,2,1,0:T(8,128)S(1)}, f32[4,3,2,4,1,8,32]{6,5,3,4,2,1,0:T(8,128)S(1)}, u32[]{:S(2)}, u32[]{:S(2)}) collective-permute-start(f32[4,3,2,4,1,8,32]{6,5,3,4,2,1,0:T(8,128)S(1)} %pad_maximum_fusion.6), channel_id=1, source_target_pairs={{4,0},{8,4},{12,8},{16,12},{20,16},{24,20},{28,24},{32,28},{36,32}... | collective-permute-start | bytes 294920 | tf_op jit(solution)/shard_map/ppermute | solution.py:40
  145.8 8.7 %collective-permute-start.17 = (f32[4,3,2,4,1,8,32]{6,5,3,4,2,1,0:T(8,128)S(1)}, f32[4,3,2,4,1,8,32]{6,5,3,4,2,1,0:T(8,128)S(1)}, u32[]{:S(2)}, u32[]{:S(2)}) collective-permute-start(f32[4,3,2,4,1,8,32]{6,5,3,4,2,1,0:T(8,128)S(1)} %pad_maximum_fusion.6), channel_id=1, source_target_pairs={{0,4},{4,8},{8,12},{12,16},{16,20},{20,24},{24,28},{28,32},{32,36}... | collective-permute-start | bytes 294920 | tf_op jit(solution)/shard_map/ppermute | solution.py:37
  154.7 11.1 %collective-permute-start.20 = (f32[4,3,2,4,3,1,32]{6,5,3,4,2,1,0:T(1,128)S(1)}, f32[4,3,2,4,3,1,32]{6,5,3,4,2,1,0:T(1,128)S(1)}, u32[]{:S(2)}, u32[]{:S(2)}) collective-permute-start(f32[4,3,2,4,3,1,32]{6,5,3,4,2,1,0:T(1,128)S(1)} %get-tuple-element.21), channel_id=1, source_target_pairs={{1,0},{2,1},{3,2},{0,3},{5,4},{6,5},{7,6},{4,7},{9,8},{10,9},{11,1... | collective-permute-start | bytes 110600 | tf_op jit(solution)/shard_map/ppermute | solution.py:40
  162.0 9.5 %collective-permute-start.19 = (f32[4,3,2,4,3,1,32]{6,5,3,4,2,1,0:T(1,128)S(1)}, f32[4,3,2,4,3,1,32]{6,5,3,4,2,1,0:T(1,128)S(1)}, u32[]{:S(2)}, u32[]{:S(2)}) collective-permute-start(f32[4,3,2,4,3,1,32]{6,5,3,4,2,1,0:T(1,128)S(1)} %get-tuple-element.20), channel_id=1, source_target_pairs={{0,1},{1,2},{2,3},{3,0},{4,5},{5,6},{6,7},{7,4},{8,9},{9,10},{10,1... | collective-permute-start | bytes 110600 | tf_op jit(solution)/shard_map/ppermute | solution.py:37
  177.3 7.6 %collective-permute-start.22 = (f32[4,3,2,1,1,8,32]{6,5,3,4,2,1,0:T(8,128)S(1)}, f32[4,3,2,1,1,8,32]{6,5,3,4,2,1,0:T(8,128)S(1)}, u32[]{:S(2)}, u32[]{:S(2)}) collective-permute-start(f32[4,3,2,1,1,8,32]{6,5,3,4,2,1,0:T(8,128)S(1)} %get-tuple-element.171), channel_id=1, source_target_pairs={{64,0},{128,64},{192,128},{256,192},{320,256},{384,320},{448,384},... | collective-permute-start | bytes 73736 | tf_op jit(solution)/shard_map/ppermute | solution.py:40
  179.2 12.6 %collective-permute-start.21 = (f32[4,3,2,1,1,8,32]{6,5,3,4,2,1,0:T(8,128)S(1)}, f32[4,3,2,1,1,8,32]{6,5,3,4,2,1,0:T(8,128)S(1)}, u32[]{:S(2)}, u32[]{:S(2)}) collective-permute-start(f32[4,3,2,1,1,8,32]{6,5,3,4,2,1,0:T(8,128)S(1)} %get-tuple-element.170), channel_id=1, source_target_pairs={{0,64},{64,128},{128,192},{192,256},{256,320},{320,384},{384,448},... | collective-permute-start | bytes 73736 | tf_op jit(solution)/shard_map/ppermute | solution.py:37
  191.8 10.9 %collective-permute-start.24 = (f32[4,3,2,4,1,8,32]{6,5,3,4,2,1,0:T(8,128)S(1)}, f32[4,3,2,4,1,8,32]{6,5,3,4,2,1,0:T(8,128)S(1)}, u32[]{:S(2)}, u32[]{:S(2)}) collective-permute-start(f32[4,3,2,4,1,8,32]{6,5,3,4,2,1,0:T(8,128)S(1)} %pad_maximum_fusion.7), channel_id=1, source_target_pairs={{4,0},{8,4},{12,8},{16,12},{20,16},{24,20},{28,24},{32,28},{36,32}... | collective-permute-start | bytes 294920 | tf_op jit(solution)/shard_map/ppermute | solution.py:40
  192.8 9.9 %collective-permute-start.23 = (f32[4,3,2,4,1,8,32]{6,5,3,4,2,1,0:T(8,128)S(1)}, f32[4,3,2,4,1,8,32]{6,5,3,4,2,1,0:T(8,128)S(1)}, u32[]{:S(2)}, u32[]{:S(2)}) collective-permute-start(f32[4,3,2,4,1,8,32]{6,5,3,4,2,1,0:T(8,128)S(1)} %pad_maximum_fusion.7), channel_id=1, source_target_pairs={{0,4},{4,8},{8,12},{12,16},{16,20},{20,24},{24,28},{28,32},{32,36}... | collective-permute-start | bytes 294920 | tf_op jit(solution)/shard_map/ppermute | solution.py:37
  202.9 9.7 %collective-permute-start.26 = (f32[4,3,2,4,3,1,32]{6,5,3,4,2,1,0:T(1,128)S(1)}, f32[4,3,2,4,3,1,32]{6,5,3,4,2,1,0:T(1,128)S(1)}, u32[]{:S(2)}, u32[]{:S(2)}) collective-permute-start(f32[4,3,2,4,3,1,32]{6,5,3,4,2,1,0:T(1,128)S(1)} %get-tuple-element.19), channel_id=1, source_target_pairs={{1,0},{2,1},{3,2},{0,3},{5,4},{6,5},{7,6},{4,7},{9,8},{10,9},{11,1... | collective-permute-start | bytes 110600 | tf_op jit(solution)/shard_map/ppermute | solution.py:40
  208.9 9.5 %collective-permute-start.25 = (f32[4,3,2,4,3,1,32]{6,5,3,4,2,1,0:T(1,128)S(1)}, f32[4,3,2,4,3,1,32]{6,5,3,4,2,1,0:T(1,128)S(1)}, u32[]{:S(2)}, u32[]{:S(2)}) collective-permute-start(f32[4,3,2,4,3,1,32]{6,5,3,4,2,1,0:T(1,128)S(1)} %get-tuple-element.18), channel_id=1, source_target_pairs={{0,1},{1,2},{2,3},{3,0},{4,5},{5,6},{6,7},{7,4},{8,9},{9,10},{10,1... | collective-permute-start | bytes 110600 | tf_op jit(solution)/shard_map/ppermute | solution.py:37
  (6 other events, 14.2 us)
where the time goes:
time: 225 us; the launch traced here: 223 us
  starting transfers between devices  93.1 us (41%)
  waiting for transfers between devices  78.5 us (35%)
  other arithmetic  35.5 us (16%)
  local copies, waits for them, and re-layouts  11.5 us (5%)
  between operations  4.86 us (2%)
    ppermute x12, starting transfers between devices, padded_2(): lax.ppermute(lax.slice_in_dim(block, 0, width, axis=dim), axis, backward)  52.9 us
    ppermute x12, waiting for transfers between devices, padded_2(): lax.ppermute(lax.slice_in_dim(block, block.shape[dim] - width, None, axis...  48.8 us
    ppermute x12, starting transfers between devices, padded_2(): lax.ppermute(lax.slice_in_dim(block, block.shape[dim] - width, None, axis...  31.8 us
    ppermute x12, waiting for transfers between devices, padded_2(): lax.ppermute(lax.slice_in_dim(block, 0, width, axis=dim), axis, backward)  29.6 us
    another operation x43, other arithmetic, clover_times(): jnp.stack([real_part * vector[:, 0] + imag_part * vector[:, 1], real_part...  8.66 us
    ppermute x3, starting transfers between devices, shifted(): lax.ppermute(x, axis, [(i, (i + by) % devices) for i in range(devices)])  8.38 us
    sub x32, other arithmetic, color_times(): real_out = real_out + link_real * vector_real - link_imag * vector_imag  4.78 us
  transfers between devices with their start and end apart: 27, of which 18 were waited for; matrix products, arithmetic and copies ran while one was open for 11% of the time, Pallas kernels for 0%

commit v1 on v0

v1 whole, which is shorter than its diff:
```python
import jax
import jax.numpy as jnp
from jax import lax
from jax.experimental import pallas as pl
from jax.experimental.pallas import tpu as pltpu
from jax.sharding import PartitionSpec as P

NX = 32
ITERS = 4
HOP = 0.125
DAMP = 0.8
MESH = pl.DeviceIdType.MESH
AXES = ("ta", "gz", "gy")
F32 = jnp.float32


def lanes():
    return lax.broadcasted_iota(jnp.int32, (8, 128), 1)


def rows():
    return lax.broadcasted_iota(jnp.int32, (8, 128), 0)


def roll_rows(v, by):
    return pltpu.roll(v, by % 8, 0)


def roll_lanes(v, by):
    return pltpu.roll(v, by % 128, 1)


def kernel(
    src_hbm, link_hbm, diag_hbm, off_hbm, sol_ref, res_ref,
    src, link, diag, off, u_re, u_im, c_re, c_im, c_dg, psi,
    t_out, t_in, z_out, z_in, y_out, y_in,
    load_sem, send_sem, recv_sem,
):
    place = [lax.axis_index(a) for a in AXES]
    count = [lax.axis_size(a) for a in AXES]
    ahead = [lax.rem(p + 1, n) for p, n in zip(place, count)]
    back = [lax.rem(p + n - 1, n) for p, n in zip(place, count)]

    barrier = pltpu.get_barrier_semaphore()
    for axis, up, down in zip(AXES, ahead, back):
        for to in (up, down):
            pl.semaphore_signal(barrier, inc=1, device_id={axis: to}, device_id_type=MESH)

    loads = [
        pltpu.make_async_copy(src_hbm, src, load_sem.at[0]),
        pltpu.make_async_copy(link_hbm, link, load_sem.at[1]),
        pltpu.make_async_copy(diag_hbm, diag, load_sem.at[2]),
        pltpu.make_async_copy(off_hbm, off, load_sem.at[3]),
    ]
    for load in loads:
        load.start()

    row, lane = rows(), lanes()
    upper = row < 4
    half = row % 2
    layer = (row // 2) % 2
    sign_j = jnp.where(upper, -1.0, 1.0).astype(F32)

    def times_i(v):
        return roll_rows(v, 4) * sign_j

    def spread(v):
        r = roll_rows(v, 4)
        return jnp.where(upper, v, r), jnp.where(upper, r, v)

    loads[1].wait()
    last = place[0] == count[0] - 1
    t_sign = jnp.where(jnp.logical_and(last, layer == 1), -HOP, HOP).astype(F32)
    conj = jnp.where(upper, 1.0, -1.0).astype(F32)

    def build(mu, weight):
        first = [link[6 * mu + c] for c in range(3)]
        second = [link[6 * mu + 3 + c] for c in range(3)]
        spread_first = [spread(v) for v in first]
        second_i = [times_i(v) for v in second]

        def product(a, b):
            return spread_first[a][0] * second[b] + spread_first[a][1] * second_i[b]

        for c in range(3):
            re, im = spread_first[c]
            u_re[mu, c] = re * weight
            u_im[mu, c] = im * weight
            re, im = spread(second[c])
            u_re[mu, 3 + c] = re * weight
            u_im[mu, 3 + c] = im * weight
            left, right = (c + 1) % 3, (c + 2) % 3
            third = (product(left, right) - product(right, left)) * conj
            re, im = spread(third)
            u_re[mu, 6 + c] = re * weight
            u_im[mu, 6 + c] = im * weight

    for mu in (3, 2, 1, 0):
        build(mu, t_sign if mu == 3 else HOP)

    loads[0].wait()
    for k in range(12):
        psi[k] = src[k]

    loads[2].wait()
    loads[3].wait()
    for k in range(6):
        even, odd = spread(diag[k])
        c_dg[2 * k] = even
        c_dg[2 * k + 1] = odd
    for k in range(30):
        re, im = spread(off[k])
        c_re[k] = re
        c_im[k] = im

    pl.semaphore_wait(barrier, 6)

    def remote(step, kind, way):
        out, into = ((t_out, t_in), (z_out, z_in), (y_out, y_in))[kind]
        to = (back, ahead)[way][kind]
        return pltpu.make_async_remote_copy(
            src_ref=out.at[step, way],
            dst_ref=into.at[step, way],
            send_sem=send_sem.at[step, kind, way],
            recv_sem=recv_sem.at[step, kind, way],
            device_id={AXES[kind]: to},
            device_id_type=MESH,
        )

    def multiply(mu, h, hi):
        out = []
        for spin in range(2):
            for i in range(3):
                total = None
                for j in range(3):
                    term = u_re[mu, 3 * i + j] * h[3 * spin + j] + u_im[mu, 3 * i + j] * hi[3 * spin + j]
                    total = term if total is None else total + term
                out.append(total)
        return out

    def multiply_adjoint(mu, h, hi):
        out = []
        for spin in range(2):
            for i in range(3):
                total = None
                for j in range(3):
                    term = u_re[mu, 3 * j + i] * h[3 * spin + j] - u_im[mu, 3 * j + i] * hi[3 * spin + j]
                    total = term if total is None else total + term
                out.append(total)
        return out

    def project(mu, factor, v, vi):
        def add(a, b, f):
            return a + b if f > 0 else a - b

        h, hi = [], []
        for c in range(3):
            p = [v[3 * s + c] for s in range(4)]
            q = [vi[3 * s + c] for s in range(4)]
            if mu == 0:
                h.append((add(p[0], q[3], factor), add(p[1], q[2], factor)))
                hi.append((add(q[0], p[3], -factor), add(q[1], p[2], -factor)))
            elif mu == 1:
                h.append((add(p[0], p[3], -factor), add(p[1], p[2], factor)))
                hi.append((add(q[0], q[3], -factor), add(q[1], q[2], factor)))
            elif mu == 2:
                h.append((add(p[0], q[2], factor), add(p[1], q[3], -factor)))
                hi.append((add(q[0], p[2], -factor), add(q[1], p[3], factor)))
            else:
                h.append((add(p[0], p[2], factor), add(p[1], p[3], factor)))
                hi.append((add(q[0], q[2], factor), add(q[1], q[3], factor)))
        flat = lambda pairs: [pairs[c][s] for s in range(2) for c in range(3)]
        return flat(h), flat(hi)

    def accumulate(mu, factor, h, acc, acc_i):
        def put(where, at, value, f):
            if where[at] is None:
                where[at] = value if f > 0 else -value
            else:
                where[at] = where[at] + value if f > 0 else where[at] - value

        for c in range(3):
            a, b = h[c], h[3 + c]
            put(acc, c, a, 1)
            put(acc, 3 + c, b, 1)
            if mu == 0:
                put(acc_i, c, b, -factor)
                put(acc_i, 3 + c, a, -factor)
            elif mu == 1:
                put(acc, 6 + c, b, factor)
                put(acc, 9 + c, a, -factor)
            elif mu == 2:
                put(acc_i, c, a, -factor)
                put(acc_i, 3 + c, b, factor)
            else:
                put(acc, 6 + c, a, factor)
                put(acc, 9 + c, b, factor)

    group = lane // 32
    x_place = lane % 32

    def pack_y(h):
        low = jnp.where(
            group < 2,
            jnp.where(group == 0, h[0], roll_lanes(h[1], 32)),
            jnp.where(group == 2, roll_lanes(h[2], 64), roll_lanes(h[3], 96)),
        )
        high = jnp.where(group == 0, h[4], roll_lanes(h[5], 32))
        return low, high

    def step_body(step, carry):
        v = [psi[k] for k in range(12)]
        vi = [times_i(x) for x in v]

        t_fwd, _ = project(3, -1, v, vi)
        for k in range(3):
            t_out[step, 0, k] = jnp.where(layer == 0, t_fwd[k], roll_rows(t_fwd[3 + k], 2))
        remote(step, 0, 0).start()
        h, hi = project(3, 1, v, vi)
        t_bwd = multiply_adjoint(3, h, hi)
        for k in range(3):
            t_out[step, 1, k] = jnp.where(layer == 1, t_bwd[k], roll_rows(t_bwd[3 + k], -2))
        remote(step, 0, 1).start()

        y_fwd, _ = project(1, -1, v, vi)
        low, high = pack_y(y_fwd)
        y_out[step, 0] = jnp.where(half == 0, low, roll_rows(high, 1))
        remote(step, 2, 0).start()
        h, hi = project(1, 1, v, vi)
        y_bwd = multiply_adjoint(1, h, hi)
        y_bwd = [roll_lanes(x, 32) for x in y_bwd]
        low, high = pack_y(y_bwd)
        y_out[step, 1] = jnp.where(half == 1, low, roll_rows(high, -1))
        remote(step, 2, 1).start()

        z_fwd, _ = project(2, -1, v, vi)
        for k in range(6):
            z_out[step, 0, k] = z_fwd[k]
        remote(step, 1, 0).start()
        h, hi = project(2, 1, v, vi)
        z_bwd = multiply_adjoint(2, h, hi)
        for k in range(6):
            z_out[step, 1, k] = z_bwd[k]
        remote(step, 1, 1).start()

        acc = [None] * 12
        acc_i = [None] * 6
        h, _ = project(0, -1, v, vi)
        h = [jnp.where(x_place == 31, roll_lanes(x, 31), roll_lanes(x, -1)) for x in h]
        accumulate(0, -1, multiply(0, h, [times_i(x) for x in h]), acc, acc_i)
        h, hi = project(0, 1, v, vi)
        h = multiply_adjoint(0, h, hi)
        h = [jnp.where(x_place == 0, roll_lanes(x, -31), roll_lanes(x, 1)) for x in h]
        accumulate(0, 1, h, acc, acc_i)

        for b in range(2):
            image = [c_dg[6 * b + i] * v[6 * b + i] for i in range(6)]
            pair = 15 * b
            for i in range(6):
                for j in range(i + 1, 6):
                    re, im = c_re[pair], c_im[pair]
                    image[i] = image[i] + (re * v[6 * b + j] + im * vi[6 * b + j])
                    image[j] = image[j] + (re * v[6 * b + i] - im * vi[6 * b + i])
                    pair += 1
            for i in range(6):
                rest = src[6 * b + i] - image[i]
                k = 6 * b + i
                acc[k] = rest if acc[k] is None else acc[k] + rest

        remote(step, 2, 0).wait_recv()
        got = y_in[step, 0]
        moved = roll_rows(got, 1)
        halo = [
            roll_lanes(moved, 96), roll_lanes(moved, 64), roll_lanes(moved, 32), moved,
            roll_lanes(got, 96), roll_lanes(got, 64),
        ]
        h = []
        for k in range(6):
            r = roll_lanes(y_fwd[k], -32)
            edge = jnp.where(half == 0, roll_rows(r, -1), halo[k])
            h.append(jnp.where(group == 3, edge, r))
        accumulate(1, -1, multiply(1, h, [times_i(x) for x in h]), acc, acc_i)
        remote(step, 2, 1).wait_recv()
        got = y_in[step, 1]
        moved = roll_rows(got, -1)
        halo = [
            moved, roll_lanes(moved, 96), roll_lanes(moved, 64), roll_lanes(moved, 32),
            got, roll_lanes(got, 96),
        ]
        h = []
        for k in range(6):
            r = y_bwd[k]
            edge = jnp.where(half == 1, roll_rows(r, 1), halo[k])
            h.append(jnp.where(group == 0, edge, r))
        accumulate(1, 1, h, acc, acc_i)

        remote(step, 1, 0).wait_recv()
        h = [z_in[step, 0, k] for k in range(6)]
        accumulate(2, -1, multiply(2, h, [times_i(x) for x in h]), acc, acc_i)
        remote(step, 1, 1).wait_recv()
        accumulate(2, 1, [z_in[step, 1, k] for k in range(6)], acc, acc_i)
        for k in range(6):
            acc[6 + k] = acc[6 + k] + times_i(acc_i[k])

        remote(step, 0, 0).wait_recv()
        h = []
        for k in range(6):
            got = t_in[step, 0, k % 3]
            halo = roll_rows(got, 2) if k < 3 else got
            h.append(jnp.where(layer == 0, roll_rows(t_fwd[k], -2), halo))
        accumulate(3, -1, multiply(3, h, [times_i(x) for x in h]), acc, acc_i)
        remote(step, 0, 1).wait_recv()
        h = []
        for k in range(6):
            got = t_in[step, 1, k % 3]
            halo = roll_rows(got, -2) if k < 3 else got
            h.append(jnp.where(layer == 1, roll_rows(t_bwd[k], 2), halo))
        accumulate(3, 1, h, acc, acc_i)

        for k in range(12):
            res_ref[k] = acc[k]
            psi[k] = v[k] + DAMP * acc[k]
        return carry

    lax.fori_loop(0, ITERS, step_body, 0)
    for k in range(12):
        sol_ref[k] = psi[k]

    def drain(step, carry):
        for kind in range(3):
            for way in range(2):
                remote(step, kind, way).wait_send()
        return carry

    lax.fori_loop(0, ITERS, drain, 0)


def body(source, link_rows, clover_diag, clover_off):
    src = source.reshape(12, 8, 128)
    link = link_rows.reshape(24, 8, 128)
    diag = clover_diag.reshape(6, 8, 128)
    off = clover_off.reshape(30, 8, 128)
    field = jax.ShapeDtypeStruct((12, 8, 128), F32)
    vmem = lambda *shape: pltpu.VMEM(shape + (8, 128), F32)
    solution, residual = pl.pallas_call(
        kernel,
        name="clover_steps",
        out_shape=(field, field),
        in_specs=[pl.BlockSpec(memory_space=pl.ANY)] * 4,
        out_specs=[pl.BlockSpec(memory_space=pltpu.VMEM)] * 2,
        scratch_shapes=[
            vmem(12), vmem(24), vmem(6), vmem(30),
            vmem(4, 9), vmem(4, 9), vmem(30), vmem(30), vmem(12), vmem(12),
            vmem(ITERS, 2, 3), vmem(ITERS, 2, 3),
            vmem(ITERS, 2, 6), vmem(ITERS, 2, 6),
            vmem(ITERS, 2), vmem(ITERS, 2),
            pltpu.SemaphoreType.DMA((4,)),
            pltpu.SemaphoreType.DMA((ITERS, 3, 2)),
            pltpu.SemaphoreType.DMA((ITERS, 3, 2)),
        ],
        compiler_params=pltpu.CompilerParams(collective_id=0, has_side_effects=True),
    )(src, link, diag, off)
    return solution.reshape(source.shape), residual.reshape(source.shape)


def solution(mesh):
    in_specs = (
        P(None, None, None, "ta", "gz", "gy"),
        P(None, None, None, None, "ta", "gz", "gy"),
        P(None, None, "ta", "gz", "gy"),
        P(None, None, None, "ta", "gz", "gy"),
    )
    out_specs = (P(None, None, None, "ta", "gz", "gy"), P(None, None, None, "ta", "gz", "gy"))
    return jax.shard_map(body, mesh=mesh, in_specs=in_specs, out_specs=out_specs, check_vma=False)
```

time: 225 us -> 43 us (0.19)
  the two profiles are of different devices: /device:TPU:25 before, /device:TPU:24 now
where the time goes in v1:
time: 43 us; the launch traced here: 42.8 us
  Pallas kernels  40.1 us (93%)
  local copies, waits for them, and re-layouts  2.06 us (5%)
  between operations  0.65 us (2%)
    pallas_call x1, Pallas kernels, body(): pl.pallas_call(kernel, name='clover_steps', out_shape=(field, field), in_...  40.1 us
    unnamed x4, local copies, waits for them, and re-layouts  2.06 us

profile of v1, /device:TPU:24, one launch (start us, length us, event | category | flops | bytes accessed | tf_op | source)
XLA Modules:
  0.0 42.8 jit_solution(7743378933979961298)
XLA Ops:
  0.6 40.1 %clover_steps.1 = (f32[12,8,128]{2,1,0:T(8,128)}, f32[12,8,128]{2,1,0:T(8,128)}) custom-call(f32[12,8,128]{2,1,0:T(8,128)} %bitcast.8, f32[24,8,128]{2,1,0:T(8,128)} %bitcast.7, f32[6,8,128]{2,1,0:T(8,128)} %bitcast.11, f32[30,8,128]{2,1,0:T(8,128)} %bitcast.6), custom_call_target="tpu_custom_call" | custom-call | tf_op jit(solution)/shard_map/clover_steps/pallas_call | solution.py:345
  40.7 0.0 copy-start
  40.8 1.4 %copy.10 = f32[4,3,2,2,1,256]{5,4,3,2,1,0:T(1,128)} copy(f32[4,3,2,2,1,256]{5,4,3,2,1,0:T(1,128)} %bitcast.10) | data formatting | bytes 98304
  42.2 0.0 copy-done
  42.2 0.6 %copy.11 = f32[4,3,2,2,1,256]{5,4,3,2,1,0:T(1,128)} copy(f32[4,3,2,2,1,256]{5,4,3,2,1,0:T(1,128)S(1)} %bitcast.9) | data formatting | bytes 98304
Async XLA Ops:
  40.7 1.4 %copy-start = (f32[12,8,128]{2,1,0:T(8,128)S(1)}, f32[12,8,128]{2,1,0:T(8,128)}, u32[]{:S(2)}) copy-start(f32[12,8,128]{2,1,0:T(8,128)} %get-tuple-element.5) | copy-start | bytes 147460

commit v2 on v1

--- a/solution.py
+++ b/solution.py
@@ -208,19 +208,20 @@
         high = jnp.where(group == 0, h[4], roll_lanes(h[5], 32))
         return low, high
 
-    def step_body(step, carry):
+    def send_t(step, v, vi):
+        h, _ = project(3, -1, v, vi)
+        for k in range(3):
+            t_out[step, 0, k] = jnp.where(layer == 0, h[k], roll_rows(h[3 + k], 2))
+        remote(step, 0, 0).start()
+        h, hi = project(3, 1, v, vi)
+        h = multiply_adjoint(3, h, hi)
+        for k in range(3):
+            t_out[step, 1, k] = jnp.where(layer == 1, h[k], roll_rows(h[3 + k], -2))
+        remote(step, 0, 1).start()
+
+    def step_body(step, final):
         v = [psi[k] for k in range(12)]
         vi = [times_i(x) for x in v]
-
-        t_fwd, _ = project(3, -1, v, vi)
-        for k in range(3):
-            t_out[step, 0, k] = jnp.where(layer == 0, t_fwd[k], roll_rows(t_fwd[3 + k], 2))
-        remote(step, 0, 0).start()
-        h, hi = project(3, 1, v, vi)
-        t_bwd = multiply_adjoint(3, h, hi)
-        for k in range(3):
-            t_out[step, 1, k] = jnp.where(layer == 1, t_bwd[k], roll_rows(t_bwd[3 + k], -2))
-        remote(step, 0, 1).start()
 
         y_fwd, _ = project(1, -1, v, vi)
         low, high = pack_y(y_fwd)
@@ -252,6 +253,13 @@
         h = multiply_adjoint(0, h, hi)
         h = [jnp.where(x_place == 0, roll_lanes(x, -31), roll_lanes(x, 1)) for x in h]
         accumulate(0, 1, h, acc, acc_i)
+        h, _ = project(3, -1, v, vi)
+        h = [jnp.where(layer == 0, roll_rows(x, -2), 0.0) for x in h]
+        accumulate(3, -1, multiply(3, h, [times_i(x) for x in h]), acc, acc_i)
+        h, hi = project(3, 1, v, vi)
+        h = multiply_adjoint(3, h, hi)
+        h = [jnp.where(layer == 1, roll_rows(x, 2), 0.0) for x in h]
+        accumulate(3, 1, h, acc, acc_i)
 
         for b in range(2):
             image = [c_dg[6 * b + i] * v[6 * b + i] for i in range(6)]
@@ -263,9 +271,16 @@
                     image[j] = image[j] + (re * v[6 * b + i] - im * vi[6 * b + i])
                     pair += 1
             for i in range(6):
-                rest = src[6 * b + i] - image[i]
                 k = 6 * b + i
-                acc[k] = rest if acc[k] is None else acc[k] + rest
+                acc[k] = acc[k] + (src[k] - image[i])
+
+        remote(step, 1, 0).wait_recv()
+        h = [z_in[step, 0, k] for k in range(6)]
+        accumulate(2, -1, multiply(2, h, [times_i(x) for x in h]), acc, acc_i)
+        remote(step, 1, 1).wait_recv()
+        accumulate(2, 1, [z_in[step, 1, k] for k in range(6)], acc, acc_i)
+        for k in range(6):
+            acc[6 + k] = acc[6 + k] + times_i(acc_i[k])
 
         remote(step, 2, 0).wait_recv()
         got = y_in[step, 0]
@@ -294,37 +309,42 @@
             h.append(jnp.where(group == 0, edge, r))
         accumulate(1, 1, h, acc, acc_i)
 
-        remote(step, 1, 0).wait_recv()
-        h = [z_in[step, 0, k] for k in range(6)]
-        accumulate(2, -1, multiply(2, h, [times_i(x) for x in h]), acc, acc_i)
-        remote(step, 1, 1).wait_recv()
-        accumulate(2, 1, [z_in[step, 1, k] for k in range(6)], acc, acc_i)
-        for k in range(6):
-            acc[6 + k] = acc[6 + k] + times_i(acc_i[k])
+        if not final:
+            early = [v[k] + DAMP * acc[k] for k in range(12)]
+            send_t(step + 1, early, [times_i(x) for x in early])
 
         remote(step, 0, 0).wait_recv()
         h = []
         for k in range(6):
             got = t_in[step, 0, k % 3]
             halo = roll_rows(got, 2) if k < 3 else got
-            h.append(jnp.where(layer == 0, roll_rows(t_fwd[k], -2), halo))
+            h.append(jnp.where(layer == 0, 0.0, halo))
         accumulate(3, -1, multiply(3, h, [times_i(x) for x in h]), acc, acc_i)
         remote(step, 0, 1).wait_recv()
         h = []
         for k in range(6):
             got = t_in[step, 1, k % 3]
             halo = roll_rows(got, -2) if k < 3 else got
-            h.append(jnp.where(layer == 1, roll_rows(t_bwd[k], 2), halo))
+            h.append(jnp.where(layer == 1, 0.0, halo))
         accumulate(3, 1, h, acc, acc_i)
 
         for k in range(12):
-            res_ref[k] = acc[k]
-            psi[k] = v[k] + DAMP * acc[k]
+            new = v[k] + DAMP * acc[k]
+            if final:
+                res_ref[k] = acc[k]
+                sol_ref[k] = new
+            else:
+                psi[k] = new
+
+    v = [psi[k] for k in range(12)]
+    send_t(0, v, [times_i(x) for x in v])
+
+    def loop_body(step, carry):
+        step_body(step, False)
         return carry
 
-    lax.fori_loop(0, ITERS, step_body, 0)
-    for k in range(12):
-        sol_ref[k] = psi[k]
+    lax.fori_loop(0, ITERS - 1, loop_body, 0)
+    step_body(ITERS - 1, True)
 
     def drain(step, carry):
         for kind in range(3):

time: 43 us -> 41.6 us (0.967)
  the two profiles are of different devices: /device:TPU:24 before, /device:TPU:25 now
where the time goes in v2:
time: 41.6 us; the launch traced here: 41.4 us
  Pallas kernels  38.7 us (93%)
  local copies, waits for them, and re-layouts  2.06 us (5%)
  between operations  0.65 us (2%)
    pallas_call x1, Pallas kernels, body(): pl.pallas_call(kernel, name='clover_steps', out_shape=(field, field), in_...  38.7 us
    unnamed x4, local copies, waits for them, and re-layouts  2.06 us

profile of v2, /device:TPU:25, one launch (start us, length us, event | category | flops | bytes accessed | tf_op | source)
XLA Modules:
  0.0 41.4 jit_solution(14964049889863242542)
XLA Ops:
  0.6 38.7 %clover_steps.1 = (f32[12,8,128]{2,1,0:T(8,128)}, f32[12,8,128]{2,1,0:T(8,128)}) custom-call(f32[12,8,128]{2,1,0:T(8,128)} %bitcast.8, f32[24,8,128]{2,1,0:T(8,128)} %bitcast.7, f32[6,8,128]{2,1,0:T(8,128)} %bitcast.11, f32[30,8,128]{2,1,0:T(8,128)} %bitcast.6), custom_call_target="tpu_custom_call" | custom-call | tf_op jit(solution)/shard_map/clover_steps/pallas_call | solution.py:365
  39.3 0.0 copy-start
  39.3 1.4 %copy.10 = f32[4,3,2,2,1,256]{5,4,3,2,1,0:T(1,128)} copy(f32[4,3,2,2,1,256]{5,4,3,2,1,0:T(1,128)} %bitcast.10) | data formatting | bytes 98304
  40.8 0.0 copy-done
  40.8 0.6 %copy.11 = f32[4,3,2,2,1,256]{5,4,3,2,1,0:T(1,128)} copy(f32[4,3,2,2,1,256]{5,4,3,2,1,0:T(1,128)S(1)} %bitcast.9) | data formatting | bytes 98304
Async XLA Ops:
  39.3 1.4 %copy-start = (f32[12,8,128]{2,1,0:T(8,128)S(1)}, f32[12,8,128]{2,1,0:T(8,128)}, u32[]{:S(2)}) copy-start(f32[12,8,128]{2,1,0:T(8,128)} %get-tuple-element.5) | copy-start | bytes 147460

commit v3 on v2

--- a/solution.py
+++ b/solution.py
@@ -33,19 +33,8 @@
 def kernel(
     src_hbm, link_hbm, diag_hbm, off_hbm, sol_ref, res_ref,
     src, link, diag, off, u_re, u_im, c_re, c_im, c_dg, psi,
-    t_out, t_in, z_out, z_in, y_out, y_in,
-    load_sem, send_sem, recv_sem,
+    out, into, load_sem, send_sem, t_sem, z_sem, y_sem,
 ):
-    place = [lax.axis_index(a) for a in AXES]
-    count = [lax.axis_size(a) for a in AXES]
-    ahead = [lax.rem(p + 1, n) for p, n in zip(place, count)]
-    back = [lax.rem(p + n - 1, n) for p, n in zip(place, count)]
-
-    barrier = pltpu.get_barrier_semaphore()
-    for axis, up, down in zip(AXES, ahead, back):
-        for to in (up, down):
-            pl.semaphore_signal(barrier, inc=1, device_id={axis: to}, device_id_type=MESH)
-
     loads = [
         pltpu.make_async_copy(src_hbm, src, load_sem.at[0]),
         pltpu.make_async_copy(link_hbm, link, load_sem.at[1]),
@@ -54,6 +43,16 @@
     ]
     for load in loads:
         load.start()
+
+    place = [lax.axis_index(a) for a in AXES]
+    count = [lax.axis_size(a) for a in AXES]
+    ahead = [jnp.where(p == n - 1, 0, p + 1) for p, n in zip(place, count)]
+    back = [jnp.where(p == 0, n - 1, p - 1) for p, n in zip(place, count)]
+
+    barrier = pltpu.get_barrier_semaphore()
+    for axis, up, down in zip(AXES, ahead, back):
+        for to in (up, down):
+            pl.semaphore_signal(barrier, inc=1, device_id={axis: to}, device_id_type=MESH)
 
     row, lane = rows(), lanes()
     upper = row < 4
@@ -95,37 +94,20 @@
             u_re[mu, 6 + c] = re * weight
             u_im[mu, 6 + c] = im * weight
 
-    for mu in (3, 2, 1, 0):
-        build(mu, t_sign if mu == 3 else HOP)
-
-    loads[0].wait()
-    for k in range(12):
-        psi[k] = src[k]
-
-    loads[2].wait()
-    loads[3].wait()
-    for k in range(6):
-        even, odd = spread(diag[k])
-        c_dg[2 * k] = even
-        c_dg[2 * k + 1] = odd
-    for k in range(30):
-        re, im = spread(off[k])
-        c_re[k] = re
-        c_im[k] = im
-
-    pl.semaphore_wait(barrier, 6)
-
     def remote(step, kind, way):
-        out, into = ((t_out, t_in), (z_out, z_in), (y_out, y_in))[kind]
-        to = (back, ahead)[way][kind]
+        part = pl.ds((0, 3, 9)[kind], (3, 6, 1)[kind])
         return pltpu.make_async_remote_copy(
-            src_ref=out.at[step, way],
-            dst_ref=into.at[step, way],
-            send_sem=send_sem.at[step, kind, way],
-            recv_sem=recv_sem.at[step, kind, way],
-            device_id={AXES[kind]: to},
+            src_ref=out.at[step, way, part],
+            dst_ref=into.at[step, way, part],
+            send_sem=send_sem,
+            recv_sem=(t_sem.at[step, way], z_sem.at[step], y_sem.at[step])[kind],
+            device_id={AXES[kind]: (back, ahead)[way][kind]},
             device_id_type=MESH,
         )
+
+    def wait_both(step, kind):
+        part = into.at[step, :, pl.ds((0, 3, 9)[kind], (3, 6, 1)[kind])]
+        pltpu.make_async_copy(part, part, (None, z_sem.at[step], y_sem.at[step])[kind]).wait()
 
     def multiply(mu, h, hi):
         out = []
@@ -211,12 +193,12 @@
     def send_t(step, v, vi):
         h, _ = project(3, -1, v, vi)
         for k in range(3):
-            t_out[step, 0, k] = jnp.where(layer == 0, h[k], roll_rows(h[3 + k], 2))
+            out[step, 0, k] = jnp.where(layer == 0, h[k], roll_rows(h[3 + k], 2))
         remote(step, 0, 0).start()
         h, hi = project(3, 1, v, vi)
         h = multiply_adjoint(3, h, hi)
         for k in range(3):
-            t_out[step, 1, k] = jnp.where(layer == 1, h[k], roll_rows(h[3 + k], -2))
+            out[step, 1, k] = jnp.where(layer == 1, h[k], roll_rows(h[3 + k], -2))
         remote(step, 0, 1).start()
 
     def step_body(step, final):
@@ -225,23 +207,23 @@
 
         y_fwd, _ = project(1, -1, v, vi)
         low, high = pack_y(y_fwd)
-        y_out[step, 0] = jnp.where(half == 0, low, roll_rows(high, 1))
+        out[step, 0, 9] = jnp.where(half == 0, low, roll_rows(high, 1))
         remote(step, 2, 0).start()
         h, hi = project(1, 1, v, vi)
         y_bwd = multiply_adjoint(1, h, hi)
         y_bwd = [roll_lanes(x, 32) for x in y_bwd]
         low, high = pack_y(y_bwd)
-        y_out[step, 1] = jnp.where(half == 1, low, roll_rows(high, -1))
+        out[step, 1, 9] = jnp.where(half == 1, low, roll_rows(high, -1))
         remote(step, 2, 1).start()
 
         z_fwd, _ = project(2, -1, v, vi)
         for k in range(6):
-            z_out[step, 0, k] = z_fwd[k]
+            out[step, 0, 3 + k] = z_fwd[k]
         remote(step, 1, 0).start()
         h, hi = project(2, 1, v, vi)
         z_bwd = multiply_adjoint(2, h, hi)
         for k in range(6):
-            z_out[step, 1, k] = z_bwd[k]
+            out[step, 1, 3 + k] = z_bwd[k]
         remote(step, 1, 1).start()
 
         acc = [None] * 12
@@ -274,16 +256,15 @@
                 k = 6 * b + i
                 acc[k] = acc[k] + (src[k] - image[i])
 
-        remote(step, 1, 0).wait_recv()
-        h = [z_in[step, 0, k] for k in range(6)]
+        wait_both(step, 1)
+        h = [into[step, 0, 3 + k] for k in range(6)]
         accumulate(2, -1, multiply(2, h, [times_i(x) for x in h]), acc, acc_i)
-        remote(step, 1, 1).wait_recv()
-        accumulate(2, 1, [z_in[step, 1, k] for k in range(6)], acc, acc_i)
+        accumulate(2, 1, [into[step, 1, 3 + k] for k in range(6)], acc, acc_i)
         for k in range(6):
             acc[6 + k] = acc[6 + k] + times_i(acc_i[k])
 
-        remote(step, 2, 0).wait_recv()
-        got = y_in[step, 0]
+        wait_both(step, 2)
+        got = into[step, 0, 9]
         moved = roll_rows(got, 1)
         halo = [
             roll_lanes(moved, 96), roll_lanes(moved, 64), roll_lanes(moved, 32), moved,
@@ -295,8 +276,7 @@
             edge = jnp.where(half == 0, roll_rows(r, -1), halo[k])
             h.append(jnp.where(group == 3, edge, r))
         accumulate(1, -1, multiply(1, h, [times_i(x) for x in h]), acc, acc_i)
-        remote(step, 2, 1).wait_recv()
-        got = y_in[step, 1]
+        got = into[step, 1, 9]
         moved = roll_rows(got, -1)
         halo = [
             moved, roll_lanes(moved, 96), roll_lanes(moved, 64), roll_lanes(moved, 32),
@@ -316,14 +296,14 @@
         remote(step, 0, 0).wait_recv()
         h = []
         for k in range(6):
-            got = t_in[step, 0, k % 3]
+            got = into[step, 0, k % 3]
             halo = roll_rows(got, 2) if k < 3 else got
             h.append(jnp.where(layer == 0, 0.0, halo))
         accumulate(3, -1, multiply(3, h, [times_i(x) for x in h]), acc, acc_i)
         remote(step, 0, 1).wait_recv()
         h = []
         for k in range(6):
-            got = t_in[step, 1, k % 3]
+            got = into[step, 1, k % 3]
             halo = roll_rows(got, -2) if k < 3 else got
             h.append(jnp.where(layer == 1, 0.0, halo))
         accumulate(3, 1, h, acc, acc_i)
@@ -336,8 +316,26 @@
             else:
                 psi[k] = new
 
-    v = [psi[k] for k in range(12)]
+    build(3, t_sign)
+    loads[0].wait()
+    v = [src[k] for k in range(12)]
+    for k in range(12):
+        psi[k] = v[k]
+    pl.semaphore_wait(barrier, 6)
     send_t(0, v, [times_i(x) for x in v])
+
+    for mu in (1, 2, 0):
+        build(mu, HOP)
+    loads[2].wait()
+    loads[3].wait()
+    for k in range(6):
+        even, odd = spread(diag[k])
+        c_dg[2 * k] = even
+        c_dg[2 * k + 1] = odd
+    for k in range(30):
+        re, im = spread(off[k])
+        c_re[k] = re
+        c_im[k] = im
 
     def loop_body(step, carry):
         step_body(step, False)
@@ -346,13 +344,7 @@
     lax.fori_loop(0, ITERS - 1, loop_body, 0)
     step_body(ITERS - 1, True)
 
-    def drain(step, carry):
-        for kind in range(3):
-            for way in range(2):
-                remote(step, kind, way).wait_send()
-        return carry
-
-    lax.fori_loop(0, ITERS, drain, 0)
+    pltpu.make_async_copy(out, out, send_sem).wait()
 
 
 def body(source, link_rows, clover_diag, clover_off):
@@ -371,12 +363,12 @@
         scratch_shapes=[
             vmem(12), vmem(24), vmem(6), vmem(30),
             vmem(4, 9), vmem(4, 9), vmem(30), vmem(30), vmem(12), vmem(12),
-            vmem(ITERS, 2, 3), vmem(ITERS, 2, 3),
-            vmem(ITERS, 2, 6), vmem(ITERS, 2, 6),
-            vmem(ITERS, 2), vmem(ITERS, 2),
+            vmem(ITERS, 2, 10), vmem(ITERS, 2, 10),
             pltpu.SemaphoreType.DMA((4,)),
-            pltpu.SemaphoreType.DMA((ITERS, 3, 2)),
-            pltpu.SemaphoreType.DMA((ITERS, 3, 2)),
+            pltpu.SemaphoreType.DMA,
+            pltpu.SemaphoreType.DMA((ITERS, 2)),
+            pltpu.SemaphoreType.DMA((ITERS,)),
+            pltpu.SemaphoreType.DMA((ITERS,)),
         ],
         compiler_params=pltpu.CompilerParams(collective_id=0, has_side_effects=True),
     )(src, link, diag, off)

time: 41.6 us -> 41.3 us (level)
  no operation moved by 1% of the time
where the time goes in v3:
time: 41.3 us; the launch traced here: 41 us
  Pallas kernels  38.3 us (93%)
  local copies, waits for them, and re-layouts  2.06 us (5%)
  between operations  0.65 us (2%)
    pallas_call x1, Pallas kernels, body(): pl.pallas_call(kernel, name='clover_steps', out_shape=(field, field), in_...  38.3 us
    unnamed x4, local copies, waits for them, and re-layouts  2.06 us

profile of v3, /device:TPU:25, one launch (start us, length us, event | category | flops | bytes accessed | tf_op | source)
XLA Modules:
  0.0 41.0 jit_solution(8931282177937784591)
XLA Ops:
  0.6 38.3 %clover_steps.1 = (f32[12,8,128]{2,1,0:T(8,128)}, f32[12,8,128]{2,1,0:T(8,128)}) custom-call(f32[12,8,128]{2,1,0:T(8,128)} %bitcast.8, f32[24,8,128]{2,1,0:T(8,128)} %bitcast.7, f32[6,8,128]{2,1,0:T(8,128)} %bitcast.11, f32[30,8,128]{2,1,0:T(8,128)} %bitcast.6), custom_call_target="tpu_custom_call" | custom-call | tf_op jit(solution)/shard_map/clover_steps/pallas_call | solution.py:357
  39.0 0.0 copy-start
  39.0 1.4 %copy.10 = f32[4,3,2,2,1,256]{5,4,3,2,1,0:T(1,128)} copy(f32[4,3,2,2,1,256]{5,4,3,2,1,0:T(1,128)} %bitcast.10) | data formatting | bytes 98304
  40.4 0.0 copy-done
  40.4 0.6 %copy.11 = f32[4,3,2,2,1,256]{5,4,3,2,1,0:T(1,128)} copy(f32[4,3,2,2,1,256]{5,4,3,2,1,0:T(1,128)S(1)} %bitcast.9) | data formatting | bytes 98304
Async XLA Ops:
  39.0 1.4 %copy-start = (f32[12,8,128]{2,1,0:T(8,128)S(1)}, f32[12,8,128]{2,1,0:T(8,128)}, u32[]{:S(2)}) copy-start(f32[12,8,128]{2,1,0:T(8,128)} %get-tuple-element.5) | copy-start | bytes 147460

commit v4 on v3

--- a/solution.py
+++ b/solution.py
@@ -347,12 +347,23 @@
     pltpu.make_async_copy(out, out, send_sem).wait()
 
 
+def store(sol_ref, res_ref, sol_hbm, res_hbm, sem):
+    copies = [
+        pltpu.make_async_copy(sol_ref, sol_hbm, sem.at[0]),
+        pltpu.make_async_copy(res_ref, res_hbm, sem.at[1]),
+    ]
+    for copy in copies:
+        copy.start()
+    for copy in copies:
+        copy.wait()
+
+
 def body(source, link_rows, clover_diag, clover_off):
     src = source.reshape(12, 8, 128)
     link = link_rows.reshape(24, 8, 128)
     diag = clover_diag.reshape(6, 8, 128)
     off = clover_off.reshape(30, 8, 128)
-    field = jax.ShapeDtypeStruct((12, 8, 128), F32)
+    field = pltpu.VMEM((12, 8, 128), F32)
     vmem = lambda *shape: pltpu.VMEM(shape + (8, 128), F32)
     solution, residual = pl.pallas_call(
         kernel,
@@ -372,6 +383,15 @@
         ],
         compiler_params=pltpu.CompilerParams(collective_id=0, has_side_effects=True),
     )(src, link, diag, off)
+    field = jax.ShapeDtypeStruct((12, 8, 128), F32)
+    solution, residual = pl.pallas_call(
+        store,
+        name="store",
+        out_shape=(field, field),
+        in_specs=[pl.BlockSpec(memory_space=pltpu.VMEM)] * 2,
+        out_specs=[pl.BlockSpec(memory_space=pl.ANY)] * 2,
+        scratch_shapes=[pltpu.SemaphoreType.DMA((2,))],
+    )(*(pltpu.with_memory_space_constraint(x, pltpu.VMEM) for x in (solution, residual)))
     return solution.reshape(source.shape), residual.reshape(source.shape)
 
 

time: 41.3 us -> 39.2 us (0.949)
  local copies, waits for them, and re-layouts: 2.06 us -> 0 us
    unnamed x4 -> x0, local copies, waits for them, and re-layouts: 2.06 us -> none
    pallas_call x0 -> x1, Pallas kernels: none -> 0.66 us  [body(): pl.pallas_call(store, name='store', out_shape=(field, field), in_specs=[p...]
    pallas_call x1, Pallas kernels: 38.3 us -> 37.7 us  [body(): pl.pallas_call(kernel, name='clover_steps', out_shape=(field, field), in_...]
where the time goes in v4:
time: 39.2 us; the launch traced here: 39 us
  Pallas kernels  38.4 us (98%)
  between operations  0.64 us (2%)
    pallas_call x1, Pallas kernels, body(): pl.pallas_call(kernel, name='clover_steps', out_shape=(field, field), in_...  37.7 us

profile of v4, /device:TPU:25, one launch (start us, length us, event | category | flops | bytes accessed | tf_op | source)
XLA Modules:
  0.0 39.0 jit_solution(13180233192846564952)
XLA Ops:
  0.6 37.7 %clover_steps.1 = (f32[12,8,128]{2,1,0:T(8,128)S(1)}, f32[12,8,128]{2,1,0:T(8,128)S(1)}) custom-call(f32[12,8,128]{2,1,0:T(8,128)} %bitcast.8, f32[24,8,128]{2,1,0:T(8,128)} %bitcast.7, f32[6,8,128]{2,1,0:T(8,128)} %bitcast.9, f32[30,8,128]{2,1,0:T(8,128)} %bitcast.6), custom_call_target="tpu_custom_call" | custom-call | tf_op jit(solution)/shard_map/clover_steps/pallas_call | solution.py:368
  38.4 0.7 %store.1 = (f32[12,8,128]{2,1,0:T(8,128)}, f32[12,8,128]{2,1,0:T(8,128)}) custom-call(f32[12,8,128]{2,1,0:T(8,128)S(1)} %get-tuple-element.6.sol_ref, f32[12,8,128]{2,1,0:T(8,128)S(1)} %get-tuple-element.7.res_ref), custom_call_target="tpu_custom_call" | custom-call | tf_op jit(solution)/shard_map/store/pallas_call | solution.py:387

commit v5 on v4

--- a/solution.py
+++ b/solution.py
@@ -11,6 +11,7 @@
 DAMP = 0.8
 MESH = pl.DeviceIdType.MESH
 AXES = ("ta", "gz", "gy")
+GROUP = 4
 F32 = jnp.float32
 
 
@@ -32,8 +33,9 @@
 
 def kernel(
     src_hbm, link_hbm, diag_hbm, off_hbm, sol_ref, res_ref,
-    src, link, diag, off, u_re, u_im, c_re, c_im, c_dg, psi,
-    out, into, load_sem, send_sem, t_sem, z_sem, y_sem,
+    src, link, diag, off, u_re, u_im, c_re, c_im, c_dg, psi, y_fwd, y_bwd,
+    out, into, park, load_sem, send_sem, t_sem, z_sem, y_sem,
+    ok_sem, park_in, park_ok, park_send,
 ):
     loads = [
         pltpu.make_async_copy(src_hbm, src, load_sem.at[0]),
@@ -49,10 +51,42 @@
     ahead = [jnp.where(p == n - 1, 0, p + 1) for p, n in zip(place, count)]
     back = [jnp.where(p == 0, n - 1, p - 1) for p, n in zip(place, count)]
 
+    ta, gz, gy = place
+    n_ta, n_gz, n_gy = count
+
+    def upward(axis, p):
+        return p < (n_ta - 2, n_gz // 2, n_gy - 1)[axis]
+
+    hears = [(upward(a, back[a]), jnp.logical_not(upward(a, place[a]))) for a in range(3)]
+    calls = [tuple(jnp.logical_not(h) for h in pair) for pair in hears]
+    far = (lax.rem(ta, GROUP) == 0, lax.rem(ta, GROUP) == GROUP - 1)
+    first, final_ta = ta == 0, ta == n_ta - 1
+    holder = jnp.logical_and(ta == GROUP - 1, gy == 0)
+
+    def beside(axis, way):
+        return {AXES[axis]: (back, ahead)[way][axis]}
+
     barrier = pltpu.get_barrier_semaphore()
-    for axis, up, down in zip(AXES, ahead, back):
-        for to in (up, down):
-            pl.semaphore_signal(barrier, inc=1, device_id={axis: to}, device_id_type=MESH)
+
+    def call(axis, way):
+        @pl.when(calls[axis][way])
+        def _():
+            pl.semaphore_signal(barrier, inc=1, device_id=beside(axis, way), device_id_type=MESH)
+
+    for axis in range(3):
+        for way in range(2):
+            call(axis, way)
+
+    @pl.when(holder)
+    def _():
+        for g in range(n_gy):
+            for t in (0, n_ta - 1):
+                pl.semaphore_signal(barrier, inc=1, device_id={"ta": t, "gy": g}, device_id_type=MESH)
+
+    expected = jnp.logical_or(first, final_ta).astype(jnp.int32)
+    for pair in hears:
+        for h in pair:
+            expected = expected + h.astype(jnp.int32)
 
     row, lane = rows(), lanes()
     upper = row < 4
@@ -100,14 +134,14 @@
             src_ref=out.at[step, way, part],
             dst_ref=into.at[step, way, part],
             send_sem=send_sem,
-            recv_sem=(t_sem.at[step, way], z_sem.at[step], y_sem.at[step])[kind],
+            recv_sem=(t_sem.at[step, way], z_sem.at[step % 2], y_sem.at[step % 2])[kind],
             device_id={AXES[kind]: (back, ahead)[way][kind]},
             device_id_type=MESH,
         )
 
     def wait_both(step, kind):
         part = into.at[step, :, pl.ds((0, 3, 9)[kind], (3, 6, 1)[kind])]
-        pltpu.make_async_copy(part, part, (None, z_sem.at[step], y_sem.at[step])[kind]).wait()
+        pltpu.make_async_copy(part, part, (None, z_sem.at[step % 2], y_sem.at[step % 2])[kind]).wait()
 
     def multiply(mu, h, hi):
         out = []
@@ -190,41 +224,51 @@
         high = jnp.where(group == 0, h[4], roll_lanes(h[5], 32))
         return low, high
 
-    def send_t(step, v, vi):
+    def fill_t(step, v, vi, send):
         h, _ = project(3, -1, v, vi)
         for k in range(3):
             out[step, 0, k] = jnp.where(layer == 0, h[k], roll_rows(h[3 + k], 2))
-        remote(step, 0, 0).start()
+        if send:
+            remote(step, 0, 0).start()
         h, hi = project(3, 1, v, vi)
         h = multiply_adjoint(3, h, hi)
         for k in range(3):
             out[step, 1, k] = jnp.where(layer == 1, h[k], roll_rows(h[3 + k], -2))
-        remote(step, 0, 1).start()
-
-    def step_body(step, final):
+        if send:
+            remote(step, 0, 1).start()
+
+    def fill_yz(step, v, vi, send):
+        h, _ = project(1, -1, v, vi)
+        low, high = pack_y(h)
+        out[step, 0, 9] = jnp.where(half == 0, low, roll_rows(high, 1))
+        if send:
+            remote(step, 2, 0).start()
+        for k in range(6):
+            y_fwd[k] = h[k]
+        h, hi = project(1, 1, v, vi)
+        h = multiply_adjoint(1, h, hi)
+        h = [roll_lanes(x, 32) for x in h]
+        low, high = pack_y(h)
+        out[step, 1, 9] = jnp.where(half == 1, low, roll_rows(high, -1))
+        if send:
+            remote(step, 2, 1).start()
+        for k in range(6):
+            y_bwd[k] = h[k]
+        h, _ = project(2, -1, v, vi)
+        for k in range(6):
+            out[step, 0, 3 + k] = h[k]
+        if send:
+            remote(step, 1, 0).start()
+        h, hi = project(2, 1, v, vi)
+        h = multiply_adjoint(2, h, hi)
+        for k in range(6):
+            out[step, 1, 3 + k] = h[k]
+        if send:
+            remote(step, 1, 1).start()
+
+    def step_body(step, begin, final):
         v = [psi[k] for k in range(12)]
         vi = [times_i(x) for x in v]
-
-        y_fwd, _ = project(1, -1, v, vi)
-        low, high = pack_y(y_fwd)
-        out[step, 0, 9] = jnp.where(half == 0, low, roll_rows(high, 1))
-        remote(step, 2, 0).start()
-        h, hi = project(1, 1, v, vi)
-        y_bwd = multiply_adjoint(1, h, hi)
-        y_bwd = [roll_lanes(x, 32) for x in y_bwd]
-        low, high = pack_y(y_bwd)
-        out[step, 1, 9] = jnp.where(half == 1, low, roll_rows(high, -1))
-        remote(step, 2, 1).start()
-
-        z_fwd, _ = project(2, -1, v, vi)
-        for k in range(6):
-            out[step, 0, 3 + k] = z_fwd[k]
-        remote(step, 1, 0).start()
-        h, hi = project(2, 1, v, vi)
-        z_bwd = multiply_adjoint(2, h, hi)
-        for k in range(6):
-            out[step, 1, 3 + k] = z_bwd[k]
-        remote(step, 1, 1).start()
 
         acc = [None] * 12
         acc_i = [None] * 6
@@ -289,9 +333,19 @@
             h.append(jnp.where(group == 0, edge, r))
         accumulate(1, 1, h, acc, acc_i)
 
+        if begin:
+            @pl.when(first)
+            def _():
+                pl.semaphore_wait(ok_sem.at[0, 0], 1)
+
+            @pl.when(jnp.logical_and(far[1], calls[0][1]))
+            def _():
+                pl.semaphore_wait(ok_sem.at[0, 1], 1)
+                remote(0, 0, 1).start()
+
         if not final:
             early = [v[k] + DAMP * acc[k] for k in range(12)]
-            send_t(step + 1, early, [times_i(x) for x in early])
+            fill_t(step + 1, early, [times_i(x) for x in early], True)
 
         remote(step, 0, 0).wait_recv()
         h = []
@@ -308,24 +362,86 @@
             h.append(jnp.where(layer == 1, 0.0, halo))
         accumulate(3, 1, h, acc, acc_i)
 
-        for k in range(12):
-            new = v[k] + DAMP * acc[k]
-            if final:
+        new = [v[k] + DAMP * acc[k] for k in range(12)]
+        if final:
+            for k in range(12):
                 res_ref[k] = acc[k]
-                sol_ref[k] = new
-            else:
-                psi[k] = new
+                sol_ref[k] = new[k]
+        else:
+            for k in range(12):
+                psi[k] = new[k]
+            fill_yz(step + 1, new, [times_i(x) for x in new], True)
 
     build(3, t_sign)
     loads[0].wait()
     v = [src[k] for k in range(12)]
+    vi = [times_i(x) for x in v]
     for k in range(12):
         psi[k] = v[k]
-    pl.semaphore_wait(barrier, 6)
-    send_t(0, v, [times_i(x) for x in v])
-
+    fill_t(0, v, vi, False)
     for mu in (1, 2, 0):
         build(mu, HOP)
+    fill_yz(0, v, vi, False)
+    pl.semaphore_wait(barrier, expected)
+
+    def answer(axis, way):
+        @pl.when(hears[axis][way])
+        def _():
+            pl.semaphore_signal(
+                ok_sem.at[axis, 1 - way], inc=1, device_id=beside(axis, way), device_id_type=MESH
+            )
+
+    for axis in range(3):
+        for way in range(2):
+            answer(axis, way)
+
+    @pl.when(final_ta)
+    def _():
+        pl.semaphore_signal(
+            park_ok.at[gy], inc=1, device_id={"ta": GROUP - 1, "gy": 0}, device_id_type=MESH
+        )
+
+    def open_to(kind, way):
+        @pl.when(calls[kind][way])
+        def _():
+            pl.semaphore_wait(ok_sem.at[kind, way], 1)
+
+        remote(0, kind, way).start()
+
+    for way in range(2):
+        @pl.when(jnp.logical_and(far[way], hears[0][way]))
+        def _(way=way):
+            remote(0, 0, way).start()
+
+    @pl.when(first)
+    def _():
+        pltpu.make_async_remote_copy(
+            src_ref=out.at[0, 0, pl.ds(0, 3)],
+            dst_ref=park.at[gy],
+            send_sem=send_sem,
+            recv_sem=park_in.at[gy],
+            device_id={"ta": GROUP - 1, "gy": 0},
+            device_id_type=MESH,
+        ).start()
+
+    for kind in (2, 1):
+        for way in range(2):
+            open_to(kind, way)
+    for way in range(2):
+        @pl.when(jnp.logical_not(far[way]))
+        def _(way=way):
+            open_to(0, way)
+
+    def hand_on(g):
+        return pltpu.make_async_remote_copy(
+            src_ref=park.at[g],
+            dst_ref=into.at[0, 0, pl.ds(0, 3)],
+            send_sem=park_send,
+            recv_sem=t_sem.at[0, 0],
+            device_id={"ta": n_ta - 1, "gy": g},
+            device_id_type=MESH,
+        )
+
     loads[2].wait()
     loads[3].wait()
     for k in range(6):
@@ -337,12 +453,25 @@
         c_re[k] = re
         c_im[k] = im
 
+    step_body(0, True, False)
+
+    @pl.when(holder)
+    def _():
+        for g in range(n_gy):
+            pltpu.make_async_copy(park.at[g], park.at[g], park_in.at[g]).wait()
+            pl.semaphore_wait(park_ok.at[g], 1)
+            hand_on(g).start()
+
     def loop_body(step, carry):
-        step_body(step, False)
+        step_body(step, False, False)
         return carry
 
-    lax.fori_loop(0, ITERS - 1, loop_body, 0)
-    step_body(ITERS - 1, True)
+    lax.fori_loop(1, ITERS - 1, loop_body, 0)
+    step_body(ITERS - 1, False, True)
+
+    @pl.when(holder)
+    def _():
+        pltpu.make_async_copy(park, park, park_send).wait()
 
     pltpu.make_async_copy(out, out, send_sem).wait()
 
@@ -364,6 +493,7 @@
     diag = clover_diag.reshape(6, 8, 128)
     off = clover_off.reshape(30, 8, 128)
     field = pltpu.VMEM((12, 8, 128), F32)
+    n_gy = lax.axis_size("gy")
     vmem = lambda *shape: pltpu.VMEM(shape + (8, 128), F32)
     solution, residual = pl.pallas_call(
         kernel,
@@ -373,13 +503,17 @@
         out_specs=[pl.BlockSpec(memory_space=pltpu.VMEM)] * 2,
         scratch_shapes=[
             vmem(12), vmem(24), vmem(6), vmem(30),
-            vmem(4, 9), vmem(4, 9), vmem(30), vmem(30), vmem(12), vmem(12),
-            vmem(ITERS, 2, 10), vmem(ITERS, 2, 10),
+            vmem(4, 9), vmem(4, 9), vmem(30), vmem(30), vmem(12), vmem(12), vmem(6), vmem(6),
+            vmem(ITERS, 2, 10), vmem(ITERS, 2, 10), vmem(n_gy, 3),
             pltpu.SemaphoreType.DMA((4,)),
             pltpu.SemaphoreType.DMA,
             pltpu.SemaphoreType.DMA((ITERS, 2)),
-            pltpu.SemaphoreType.DMA((ITERS,)),
-            pltpu.SemaphoreType.DMA((ITERS,)),
+            pltpu.SemaphoreType.DMA((2,)),
+            pltpu.SemaphoreType.DMA((2,)),
+            pltpu.SemaphoreType.REGULAR((3, 2)),
+            pltpu.SemaphoreType.DMA((n_gy,)),
+            pltpu.SemaphoreType.REGULAR((n_gy,)),
+            pltpu.SemaphoreType.DMA,
         ],
         compiler_params=pltpu.CompilerParams(collective_id=0, has_side_effects=True),
     )(src, link, diag, off)

time: 39.2 us -> 36.6 us (0.934)
  the two profiles are of different devices: /device:TPU:25 before, /device:TPU:31 now
where the time goes in v5:
time: 36.6 us; the launch traced here: 36.4 us
  Pallas kernels  35.8 us (98%)
  between operations  0.64 us (2%)
    pallas_call x1, Pallas kernels, body(): pl.pallas_call(kernel, name='clover_steps', out_shape=(field, field), in_...  35.1 us

profile of v5, /device:TPU:31, one launch (start us, length us, event | category | flops | bytes accessed | tf_op | source)
XLA Modules:
  0.0 36.4 jit_solution(16081386696121831679)
XLA Ops:
  0.6 35.1 %clover_steps.1 = (f32[12,8,128]{2,1,0:T(8,128)S(1)}, f32[12,8,128]{2,1,0:T(8,128)S(1)}) custom-call(f32[12,8,128]{2,1,0:T(8,128)} %bitcast.8, f32[24,8,128]{2,1,0:T(8,128)} %bitcast.7, f32[6,8,128]{2,1,0:T(8,128)} %bitcast.9, f32[30,8,128]{2,1,0:T(8,128)} %bitcast.6), custom_call_target="tpu_custom_call" | custom-call | tf_op jit(solution)/shard_map/clover_steps/pallas_call | solution.py:498
  35.8 0.7 %store.1 = (f32[12,8,128]{2,1,0:T(8,128)}, f32[12,8,128]{2,1,0:T(8,128)}) custom-call(f32[12,8,128]{2,1,0:T(8,128)S(1)} %get-tuple-element.6.sol_ref, f32[12,8,128]{2,1,0:T(8,128)S(1)} %get-tuple-element.7.res_ref), custom_call_target="tpu_custom_call" | custom-call | tf_op jit(solution)/shard_map/store/pallas_call | solution.py:521

commit v6 on v5

--- a/solution.py
+++ b/solution.py
@@ -55,13 +55,21 @@
     n_ta, n_gz, n_gy = count
 
     def upward(axis, p):
-        return p < (n_ta - 2, n_gz // 2, n_gy - 1)[axis]
+        if axis == 1:
+            return jnp.logical_and(p % 2 == 1, p < n_gz - 1)
+        return p < (n_ta - 2, None, n_gy - 1)[axis]
 
     hears = [(upward(a, back[a]), jnp.logical_not(upward(a, place[a]))) for a in range(3)]
     calls = [tuple(jnp.logical_not(h) for h in pair) for pair in hears]
     far = (lax.rem(ta, GROUP) == 0, lax.rem(ta, GROUP) == GROUP - 1)
-    first, final_ta = ta == 0, ta == n_ta - 1
-    holder = jnp.logical_and(ta == GROUP - 1, gy == 0)
+    early = jnp.logical_or(ta == 0, ta == GROUP - 1)
+    late = jnp.logical_or(ta == n_ta - 1, ta == GROUP)
+    onward = jnp.logical_or(ta == GROUP - 1, ta == GROUP).astype(jnp.int32)
+    holds = (jnp.logical_and(ta == GROUP - 1, gy == 0), jnp.logical_and(ta == 0, gy == n_gy - 1))
+    holder_of = {
+        "ta": jnp.where(onward == 1, 0, GROUP - 1), "gy": jnp.where(onward == 1, n_gy - 1, 0)
+    }
+    ends = ((0, n_ta - 1), (GROUP - 1, GROUP))
 
     def beside(axis, way):
         return {AXES[axis]: (back, ahead)[way][axis]}
@@ -77,16 +85,33 @@
         for way in range(2):
             call(axis, way)
 
-    @pl.when(holder)
-    def _():
-        for g in range(n_gy):
-            for t in (0, n_ta - 1):
-                pl.semaphore_signal(barrier, inc=1, device_id={"ta": t, "gy": g}, device_id_type=MESH)
-
-    expected = jnp.logical_or(first, final_ta).astype(jnp.int32)
+    for way in range(2):
+        @pl.when(holds[way])
+        def _(way=way):
+            for g in range(n_gy):
+                for t in ends[way]:
+                    pl.semaphore_signal(barrier, inc=1, device_id={"ta": t, "gy": g}, device_id_type=MESH)
+
+    expected = jnp.logical_or(early, late).astype(jnp.int32)
     for pair in hears:
         for h in pair:
             expected = expected + h.astype(jnp.int32)
+    pl.semaphore_wait(barrier, expected)
+
+    def answer(axis, way):
+        @pl.when(hears[axis][way])
+        def _():
+            pl.semaphore_signal(
+                ok_sem.at[axis, 1 - way], inc=1, device_id=beside(axis, way), device_id_type=MESH
+            )
+
+    for axis in range(3):
+        for way in range(2):
+            answer(axis, way)
+
+    @pl.when(late)
+    def _():
+        pl.semaphore_signal(park_ok.at[gy], inc=1, device_id=holder_of, device_id_type=MESH)
 
     row, lane = rows(), lanes()
     upper = row < 4
@@ -224,18 +249,60 @@
         high = jnp.where(group == 0, h[4], roll_lanes(h[5], 32))
         return low, high
 
+    def leave(step, way):
+        return pltpu.make_async_remote_copy(
+            src_ref=out.at[step, way, pl.ds(0, 3)],
+            dst_ref=park.at[step, gy],
+            send_sem=send_sem,
+            recv_sem=park_in.at[step, gy],
+            device_id=holder_of,
+            device_id_type=MESH,
+        )
+
+    def hand_on(way):
+        @pl.when(holds[way])
+        def _():
+            for step in range(2):
+                for g in range(n_gy):
+                    got = park.at[step, g]
+                    pltpu.make_async_copy(got, got, park_in.at[step, g]).wait()
+                    if step == 0:
+                        pl.semaphore_wait(park_ok.at[g], 1)
+                    pltpu.make_async_remote_copy(
+                        src_ref=got,
+                        dst_ref=into.at[step, way, pl.ds(0, 3)],
+                        send_sem=park_send,
+                        recv_sem=t_sem.at[step, way],
+                        device_id={"ta": ends[way][1], "gy": g},
+                        device_id_type=MESH,
+                    ).start()
+
     def fill_t(step, v, vi, send):
         h, _ = project(3, -1, v, vi)
         for k in range(3):
             out[step, 0, k] = jnp.where(layer == 0, h[k], roll_rows(h[3 + k], 2))
         if send:
-            remote(step, 0, 0).start()
+            send(step, 0)
         h, hi = project(3, 1, v, vi)
         h = multiply_adjoint(3, h, hi)
         for k in range(3):
             out[step, 1, k] = jnp.where(layer == 1, h[k], roll_rows(h[3 + k], -2))
         if send:
-            remote(step, 0, 1).start()
+            send(step, 1)
+
+    def send_t(step, way):
+        remote(step, 0, way).start()
+
+    def send_or_leave(step, way):
+        mine = jnp.logical_and(early, onward == way)
+
+        @pl.when(jnp.logical_not(mine))
+        def _():
+            remote(step, 0, way).start()
+
+        @pl.when(mine)
+        def _():
+            leave(step, way).start()
 
     def fill_yz(step, v, vi, send):
         h, _ = project(1, -1, v, vi)
@@ -334,18 +401,16 @@
         accumulate(1, 1, h, acc, acc_i)
 
         if begin:
-            @pl.when(first)
-            def _():
-                pl.semaphore_wait(ok_sem.at[0, 0], 1)
-
-            @pl.when(jnp.logical_and(far[1], calls[0][1]))
+            @pl.when(jnp.logical_and(jnp.logical_and(far[1], calls[0][1]), jnp.logical_not(early)))
             def _():
                 pl.semaphore_wait(ok_sem.at[0, 1], 1)
                 remote(0, 0, 1).start()
 
         if not final:
-            early = [v[k] + DAMP * acc[k] for k in range(12)]
-            fill_t(step + 1, early, [times_i(x) for x in early], True)
+            part = [v[k] + DAMP * acc[k] for k in range(12)]
+            fill_t(step + 1, part, [times_i(x) for x in part], send_or_leave if begin else send_t)
+        if begin:
+            hand_on(1)
 
         remote(step, 0, 0).wait_recv()
         h = []
@@ -378,69 +443,30 @@
     vi = [times_i(x) for x in v]
     for k in range(12):
         psi[k] = v[k]
-    fill_t(0, v, vi, False)
+    fill_t(0, v, vi, None)
     for mu in (1, 2, 0):
         build(mu, HOP)
     fill_yz(0, v, vi, False)
-    pl.semaphore_wait(barrier, expected)
-
-    def answer(axis, way):
-        @pl.when(hears[axis][way])
+    def open_to(kind, way, answered):
+        near = jnp.logical_not(far[way]) if kind == 0 else True
+        side = calls[kind][way] if answered else hears[kind][way]
+
+        @pl.when(jnp.logical_and(side, near) if answered else side)
         def _():
-            pl.semaphore_signal(
-                ok_sem.at[axis, 1 - way], inc=1, device_id=beside(axis, way), device_id_type=MESH
-            )
-
-    for axis in range(3):
+            if answered:
+                pl.semaphore_wait(ok_sem.at[kind, way], 1)
+            remote(0, kind, way).start()
+
+    for kind in (0, 2, 1):
         for way in range(2):
-            answer(axis, way)
-
-    @pl.when(final_ta)
+            open_to(kind, way, False)
+
+    @pl.when(early)
     def _():
-        pl.semaphore_signal(
-            park_ok.at[gy], inc=1, device_id={"ta": GROUP - 1, "gy": 0}, device_id_type=MESH
-        )
-
-    def open_to(kind, way):
-        @pl.when(calls[kind][way])
-        def _():
-            pl.semaphore_wait(ok_sem.at[kind, way], 1)
-
-        remote(0, kind, way).start()
-
-    for way in range(2):
-        @pl.when(jnp.logical_and(far[way], hears[0][way]))
-        def _(way=way):
-            remote(0, 0, way).start()
-
-    @pl.when(first)
-    def _():
-        pltpu.make_async_remote_copy(
-            src_ref=out.at[0, 0, pl.ds(0, 3)],
-            dst_ref=park.at[gy],
-            send_sem=send_sem,
-            recv_sem=park_in.at[gy],
-            device_id={"ta": GROUP - 1, "gy": 0},
-            device_id_type=MESH,
-        ).start()
-
-    for kind in (2, 1):
-        for way in range(2):
-            open_to(kind, way)
-    for way in range(2):
-        @pl.when(jnp.logical_not(far[way]))
-        def _(way=way):
-            open_to(0, way)
-
-    def hand_on(g):
-        return pltpu.make_async_remote_copy(
-            src_ref=park.at[g],
-            dst_ref=into.at[0, 0, pl.ds(0, 3)],
-            send_sem=park_send,
-            recv_sem=t_sem.at[0, 0],
-            device_id={"ta": n_ta - 1, "gy": g},
-            device_id_type=MESH,
-        )
+        leave(0, onward).start()
+
+    for kind, way in ((1, 0), (1, 1), (0, 0), (0, 1), (2, 1), (2, 0)):
+        open_to(kind, way, True)
 
     loads[2].wait()
     loads[3].wait()
@@ -455,12 +481,11 @@
 
     step_body(0, True, False)
 
-    @pl.when(holder)
+    hand_on(0)
+
+    @pl.when(early)
     def _():
-        for g in range(n_gy):
-            pltpu.make_async_copy(park.at[g], park.at[g], park_in.at[g]).wait()
-            pl.semaphore_wait(park_ok.at[g], 1)
-            hand_on(g).start()
+        pl.semaphore_wait(ok_sem.at[0, onward], 1)
 
     def loop_body(step, carry):
         step_body(step, False, False)
@@ -469,7 +494,7 @@
     lax.fori_loop(1, ITERS - 1, loop_body, 0)
     step_body(ITERS - 1, False, True)
 
-    @pl.when(holder)
+    @pl.when(jnp.logical_or(*holds))
     def _():
         pltpu.make_async_copy(park, park, park_send).wait()
 
@@ -504,14 +529,14 @@
         scratch_shapes=[
             vmem(12), vmem(24), vmem(6), vmem(30),
             vmem(4, 9), vmem(4, 9), vmem(30), vmem(30), vmem(12), vmem(12), vmem(6), vmem(6),
-            vmem(ITERS, 2, 10), vmem(ITERS, 2, 10), vmem(n_gy, 3),
+            vmem(ITERS, 2, 10), vmem(ITERS, 2, 10), vmem(2, n_gy, 3),
             pltpu.SemaphoreType.DMA((4,)),
             pltpu.SemaphoreType.DMA,
             pltpu.SemaphoreType.DMA((ITERS, 2)),
             pltpu.SemaphoreType.DMA((2,)),
             pltpu.SemaphoreType.DMA((2,)),
             pltpu.SemaphoreType.REGULAR((3, 2)),
-            pltpu.SemaphoreType.DMA((n_gy,)),
+            pltpu.SemaphoreType.DMA((2, n_gy)),
             pltpu.SemaphoreType.REGULAR((n_gy,)),
             pltpu.SemaphoreType.DMA,
         ],

time: 36.6 us -> 35.4 us (0.967)
  the two profiles are of different devices: /device:TPU:31 before, /device:TPU:25 now
where the time goes in v6:
time: 35.4 us; the launch traced here: 35.3 us
  Pallas kernels  34.6 us (98%)
  between operations  0.64 us (2%)
    pallas_call x1, Pallas kernels, body(): pl.pallas_call(kernel, name='clover_steps', out_shape=(field, field), in_...  34 us

profile of v6, /device:TPU:25, one launch (start us, length us, event | category | flops | bytes accessed | tf_op | source)
XLA Modules:
  0.0 35.3 jit_solution(16768027796038886588)
XLA Ops:
  0.6 34.0 %clover_steps.1 = (f32[12,8,128]{2,1,0:T(8,128)S(1)}, f32[12,8,128]{2,1,0:T(8,128)S(1)}) custom-call(f32[12,8,128]{2,1,0:T(8,128)} %bitcast.8, f32[24,8,128]{2,1,0:T(8,128)} %bitcast.7, f32[6,8,128]{2,1,0:T(8,128)} %bitcast.9, f32[30,8,128]{2,1,0:T(8,128)} %bitcast.6), custom_call_target="tpu_custom_call" | custom-call | tf_op jit(solution)/shard_map/clover_steps/pallas_call | solution.py:523
  34.6 0.7 %store.1 = (f32[12,8,128]{2,1,0:T(8,128)}, f32[12,8,128]{2,1,0:T(8,128)}) custom-call(f32[12,8,128]{2,1,0:T(8,128)S(1)} %get-tuple-element.6.sol_ref, f32[12,8,128]{2,1,0:T(8,128)S(1)} %get-tuple-element.7.res_ref), custom_call_target="tpu_custom_call" | custom-call | tf_op jit(solution)/shard_map/store/pallas_call | solution.py:546

commit v7 on v6

--- a/solution.py
+++ b/solution.py
@@ -98,6 +98,10 @@
             expected = expected + h.astype(jnp.int32)
     pl.semaphore_wait(barrier, expected)
 
+    @pl.when(late)
+    def _():
+        pl.semaphore_signal(park_ok.at[gy], inc=1, device_id=holder_of, device_id_type=MESH)
+
     def answer(axis, way):
         @pl.when(hears[axis][way])
         def _():
@@ -108,10 +112,6 @@
     for axis in range(3):
         for way in range(2):
             answer(axis, way)
-
-    @pl.when(late)
-    def _():
-        pl.semaphore_signal(park_ok.at[gy], inc=1, device_id=holder_of, device_id_type=MESH)
 
     row, lane = rows(), lanes()
     upper = row < 4
@@ -487,11 +487,8 @@
     def _():
         pl.semaphore_wait(ok_sem.at[0, onward], 1)
 
-    def loop_body(step, carry):
+    for step in range(1, ITERS - 1):
         step_body(step, False, False)
-        return carry
-
-    lax.fori_loop(1, ITERS - 1, loop_body, 0)
     step_body(ITERS - 1, False, True)
 
     @pl.when(jnp.logical_or(*holds))

time: 35.4 us -> 35.4 us (level)
  no operation moved by 1% of the time
where the time goes in v7:
time: 35.4 us; the launch traced here: 35.3 us
  Pallas kernels  34.6 us (98%)
  between operations  0.64 us (2%)
    pallas_call x1, Pallas kernels, body(): pl.pallas_call(kernel, name='clover_steps', out_shape=(field, field), in_...  34 us

profile of v7, /device:TPU:25, one launch (start us, length us, event | category | flops | bytes accessed | tf_op | source)
XLA Modules:
  0.0 35.3 jit_solution(4729742356780722755)
XLA Ops:
  0.6 34.0 %clover_steps.1 = (f32[12,8,128]{2,1,0:T(8,128)S(1)}, f32[12,8,128]{2,1,0:T(8,128)S(1)}) custom-call(f32[12,8,128]{2,1,0:T(8,128)} %bitcast.8, f32[24,8,128]{2,1,0:T(8,128)} %bitcast.7, f32[6,8,128]{2,1,0:T(8,128)} %bitcast.9, f32[30,8,128]{2,1,0:T(8,128)} %bitcast.6), custom_call_target="tpu_custom_call" | custom-call | tf_op jit(solution)/shard_map/clover_steps/pallas_call | solution.py:520
  34.6 0.7 %store.1 = (f32[12,8,128]{2,1,0:T(8,128)}, f32[12,8,128]{2,1,0:T(8,128)}) custom-call(f32[12,8,128]{2,1,0:T(8,128)S(1)} %get-tuple-element.6.sol_ref, f32[12,8,128]{2,1,0:T(8,128)S(1)} %get-tuple-element.7.res_ref), custom_call_target="tpu_custom_call" | custom-call | tf_op jit(solution)/shard_map/store/pallas_call | solution.py:543

commit v8 on v7

--- a/solution.py
+++ b/solution.py
@@ -81,7 +81,7 @@
         def _():
             pl.semaphore_signal(barrier, inc=1, device_id=beside(axis, way), device_id_type=MESH)
 
-    for axis in range(3):
+    for axis in (2, 0, 1):
         for way in range(2):
             call(axis, way)
 
@@ -109,7 +109,7 @@
                 ok_sem.at[axis, 1 - way], inc=1, device_id=beside(axis, way), device_id_type=MESH
             )
 
-    for axis in range(3):
+    for axis in (2, 0, 1):
         for way in range(2):
             answer(axis, way)
 

time: 35.4 us -> 35.3 us (level)
  no operation moved by 1% of the time
where the time goes in v8:
time: 35.3 us; the launch traced here: 35.1 us
  Pallas kernels  34.5 us (98%)
  between operations  0.64 us (2%)
    pallas_call x1, Pallas kernels, body(): pl.pallas_call(kernel, name='clover_steps', out_shape=(field, field), in_...  33.8 us

profile of v8, /device:TPU:25, one launch (start us, length us, event | category | flops | bytes accessed | tf_op | source)
XLA Modules:
  0.0 35.1 jit_solution(14927068980570766179)
XLA Ops:
  0.6 33.8 %clover_steps.1 = (f32[12,8,128]{2,1,0:T(8,128)S(1)}, f32[12,8,128]{2,1,0:T(8,128)S(1)}) custom-call(f32[12,8,128]{2,1,0:T(8,128)} %bitcast.8, f32[24,8,128]{2,1,0:T(8,128)} %bitcast.7, f32[6,8,128]{2,1,0:T(8,128)} %bitcast.9, f32[30,8,128]{2,1,0:T(8,128)} %bitcast.6), custom_call_target="tpu_custom_call" | custom-call | tf_op jit(solution)/shard_map/clover_steps/pallas_call | solution.py:520
  34.5 0.7 %store.1 = (f32[12,8,128]{2,1,0:T(8,128)}, f32[12,8,128]{2,1,0:T(8,128)}) custom-call(f32[12,8,128]{2,1,0:T(8,128)S(1)} %get-tuple-element.6.sol_ref, f32[12,8,128]{2,1,0:T(8,128)S(1)} %get-tuple-element.7.res_ref), custom_call_target="tpu_custom_call" | custom-call | tf_op jit(solution)/shard_map/store/pallas_call | solution.py:543
